TPU v7x, 32 devices: a whole 2x2x4 slice. The times are simulated.
32 devices in a mesh: fluid: 8 (over z, core), struct: 4 (over y, x).
Axes of the slice: x: 2, y: 2, z: 4, core: 2. Of those that a mesh axis runs over, the one named last changes fastest.
Arguments:
- fluid_adjoint: float32 [5, 16384], P(None, ('fluid', 'struct')), may hold values from -6 to 6
- fluid_rhs: float32 [5, 16384], P(None, ('fluid', 'struct')), may hold values from -6 to 6
- diag_inverse: float32 [5, 5, 16384], P(None, None, ('fluid', 'struct'))
- face_blocks: float32 [6, 5, 5, 16384], P(None, None, None, ('fluid', 'struct')), may hold values from -0.625 to 0.625
- face_index: int32 [6, 16384], P(None, ('fluid', 'struct')), may hold values from 0 to 1023, as said below
- surface_cell: int32 [8192], P(('fluid', 'struct')), may hold values from 0 to 511, as said below
- surface_count: int32 [32], P(('fluid', 'struct')), may hold values from 32 to 256, as said below
- transfer_node: int32 [3, 8192], P(None, ('fluid', 'struct')), may hold values from 0 to 2047
- transfer_weight: float32 [3, 8192], P(None, ('fluid', 'struct')), may hold values from 0.2 to 1
- load_sens: float32 [3, 5, 8192], P(None, None, ('fluid', 'struct')), may hold values from -4 to 4
- disp_sens: float32 [5, 3, 8192], P(None, None, ('fluid', 'struct')), may hold values from -2.4 to 2.4
- struct_adjoint: float32 [12288], P('struct'), may hold values from -6 to 6
- struct_rhs: float32 [12288], P('struct'), may hold values from -6 to 6
- shell_blocks: float32 [4, 128, 9216], P(None, 'struct'), may hold values from -0.15625 to 0.15625
- shell_inverse: float32 [128, 9216], P('struct')
- shell_columns: int32 [4, 128], P(None, 'struct'), may hold values from 0 to 127
Outputs:
- fluid_out: float32 [5, 16384], P(None, ('fluid', 'struct'))
- struct_out: float32 [12288], P('struct')
Inputs may be any that keep to these rules, and one draw needn't show every extreme that they name: `face_index`: neighbour positions lie within 256 cells of the cell's own position in the extended block; the two ends of the range are taken. `surface_cell`: distinct within each block of 256 slots; every block holds the first and the last cell of the block. `surface_count`: some block has all its slots live and some has 32.
All inputs are finite; a program needn't handle non-finite values.
Results may differ from a plain program's by a relative error of at most 0.00021.
Values sent between devices are 32-bit elements; how exact they have to be, the bound alone decides.
A program may use at most 64 MiB of HBM per device.

v0:
```python
import functools

import jax
import jax.numpy as jnp
from jax import lax
from jax.experimental import pallas as pl
from jax.experimental.pallas import tpu as pltpu
from jax.sharding import PartitionSpec as P

NVAR = 5
FACES = 6
TMAP = 3
DOF = 6
BLK = 96
NB = 4
SWEEPS = 6
ITERS = 2
NPB = BLK // DOF
WIDE = (2, 4)
LANE = 128
ROWS = 8
FOLD = 384
CHUNK = 768
MESH = pl.DeviceIdType.MESH
NN = (((1,), (0,)), ((), ()))
NT = (((1,), (1,)), ((), ()))


def split(value):
    high = value.astype(jnp.bfloat16)
    rest = value - high.astype(jnp.float32)
    middle = rest.astype(jnp.bfloat16)
    low = (rest - middle.astype(jnp.float32)).astype(jnp.bfloat16)
    return high, middle, low


def dot(left, right, dims):
    return lax.dot_general(left, right, dims, preferred_element_type=jnp.float32)


def dot_left(value, table, dims):
    rows = value.shape[0]
    stacked = jnp.concatenate([p.astype(jnp.float32) for p in split(value)], axis=0)
    out = dot(stacked.astype(jnp.bfloat16), table, dims)
    return out[0:rows] + (out[rows : 2 * rows] + out[2 * rows : 3 * rows])


def dot_right(table, value, dims):
    high, middle, low = split(value)
    return dot(table, high, dims) + (dot(table, middle, dims) + dot(table, low, dims))


def iota(shape, axis):
    return lax.broadcasted_iota(jnp.int32, shape, axis)


def pad_rows(value, rows=ROWS):
    return jnp.concatenate(
        [value, jnp.zeros((rows - value.shape[0], value.shape[1]), value.dtype)], axis=0
    )


def by_block(flat, out):
    groups = flat.shape[0] * LANE // FOLD
    wide = jnp.concatenate(
        [flat[pl.ds(a, groups, stride=FOLD // LANE)] for a in range(FOLD // LANE)], axis=1
    )
    for q in range(FOLD // BLK):
        part = wide[:, q * BLK : (q + 1) * BLK]
        full = jnp.concatenate([part, jnp.zeros((groups, LANE - BLK), jnp.float32)], axis=1)
        out[pl.ds(q, groups, stride=FOLD // BLK)] = full


def kernel(
    fluid_n,
    struct_n,
    piece,
    adj_ref,
    rhs_ref,
    diag_ref,
    face_ref,
    index_ref,
    cell_ref,
    count_ref,
    node_ref,
    weight_ref,
    load_ref,
    disp_ref,
    sadj_ref,
    srhs_ref,
    blocks_ref,
    inverse_ref,
    columns_ref,
    fluid_ref,
    struct_ref,
    state,
    low_halo,
    high_halo,
    folded,
    fold_low,
    fold_high,
    bias,
    bias_low,
    bias_high,
    index_all,
    index_low,
    index_high,
    diag_t,
    cell_table,
    block_table,
    node_mask,
    blocks,
    inverse,
    expand,
    start_struct,
    right_struct,
    struct_land,
    struct_all,
    rows_x,
    terms,
    forces_out,
    forces_land,
    result,
    final_land,
    halo_send,
    halo_recv,
    once_send,
    once_recv,
    start_send,
    start_recv,
    force_send,
    force_recv,
    gather_send,
    gather_recv,
    local_sem,
):
    me_f = lax.axis_index("fluid")
    me_s = lax.axis_index("struct")
    me = me_f * struct_n + me_s
    total = fluid_n * struct_n
    cells = adj_ref.shape[1]
    half = cells // 2
    tiles = cells // LANE
    half_tiles = half // LANE
    slots = cell_ref.shape[1]
    shell_total = block_table.shape[0]
    shard_rows = start_struct.shape[0]
    my_row = me_f * piece
    base = (my_row // ROWS) * ROWS

    def dev(index):
        return (index // struct_n, index % struct_n)

    fold_low[...] = jnp.zeros_like(fold_low)
    fold_high[...] = jnp.zeros_like(fold_high)
    barrier = pltpu.get_barrier_semaphore()

    def greet(r, carry):
        pl.semaphore_signal(
            barrier, inc=1, device_id=dev((me + r) % total), device_id_type=MESH
        )
        return carry

    lax.fori_loop(1, total, greet, 0)

    local = []
    for m in range(NB):
        local.append(
            pltpu.make_async_copy(
                blocks_ref.at[m, pl.ds(pl.multiple_of(base, ROWS), ROWS)],
                blocks.at[m],
                local_sem.at[m],
            )
        )
    local.append(
        pltpu.make_async_copy(
            inverse_ref.at[pl.ds(pl.multiple_of(base, ROWS), ROWS)], inverse, local_sem.at[NB]
        )
    )
    for copy in local:
        copy.start()

    @pl.when(me == 0)
    def _():
        for ref in (low_halo, bias_low, index_low):
            ref[...] = jnp.zeros_like(ref)

    @pl.when(me == total - 1)
    def _():
        for ref in (high_halo, bias_high, index_high):
            ref[...] = jnp.zeros_like(ref)

    state[0] = pad_rows(adj_ref[...])
    index_all[...] = pad_rows(index_ref[...])
    forces_out[...] = jnp.zeros_like(forces_out)
    by_block(sadj_ref, start_struct)
    by_block(srhs_ref, right_struct)

    pl.semaphore_wait(barrier, total - 1)

    def start_copy(r):
        peer = (me_s + r) % struct_n
        return pltpu.make_async_remote_copy(
            src_ref=start_struct,
            dst_ref=struct_land.at[me_s],
            send_sem=start_send.at[r],
            recv_sem=start_recv.at[me_s],
            device_id=(me_f, peer),
            device_id_type=MESH,
        )

    for r in range(1, struct_n):
        start_copy(r).start()

    def to_low(source, landing, send, recv):
        return pltpu.make_async_remote_copy(
            src_ref=source,
            dst_ref=landing,
            send_sem=send,
            recv_sem=recv,
            device_id=dev(me - 1),
            device_id_type=MESH,
        )

    def to_high(source, landing, send, recv):
        return pltpu.make_async_remote_copy(
            src_ref=source,
            dst_ref=landing,
            send_sem=send,
            recv_sem=recv,
            device_id=dev(me + 1),
            device_id_type=MESH,
        )

    def swap_start(down, up):
        @pl.when(me > 0)
        def _():
            to_low(*down).start()

        @pl.when(me < total - 1)
        def _():
            to_high(*up).start()

    def swap_wait(down, up):
        @pl.when(me > 0)
        def _():
            to_low(*down).wait_send()
            to_high(*up).wait_recv()

        @pl.when(me < total - 1)
        def _():
            to_high(*up).wait_send()
            to_low(*down).wait_recv()

    def halo(t):
        return (
            (state.at[t], high_halo.at[t], halo_send.at[t, 0], halo_recv.at[t, 0]),
            (state.at[t], low_halo.at[t], halo_send.at[t, 1], halo_recv.at[t, 1]),
        )

    low_span, high_span = slice(0, half), slice(half, cells)

    def fold_swap():
        return (
            (folded.at[:, :, 0:NVAR, low_span], fold_high.at[:, :, 0:NVAR], once_send.at[0, 0], once_recv.at[0, 0]),
            (folded.at[:, :, 0:NVAR, high_span], fold_low.at[:, :, 0:NVAR], once_send.at[0, 1], once_recv.at[0, 1]),
        )

    def index_swap():
        return (
            (index_all.at[:, low_span], index_high, once_send.at[1, 0], once_recv.at[1, 0]),
            (index_all.at[:, high_span], index_low, once_send.at[1, 1], once_recv.at[1, 1]),
        )

    def bias_swap(i):
        n = 2 + i
        return (
            (bias.at[i, :, low_span], bias_high.at[i], once_send.at[n, 0], once_recv.at[n, 0]),
            (bias.at[i, :, high_span], bias_low.at[i], once_send.at[n, 1], once_recv.at[n, 1]),
        )

    swap_start(*halo(0))
    swap_start(*index_swap())

    for w in range(NVAR):
        for v in range(NVAR):
            diag_t[w, v : v + 1] = diag_ref[v, w : w + 1]
    for k in range(FACES):
        for u in range(NVAR):
            out = jnp.zeros((NVAR, cells), jnp.float32)
            for w in range(NVAR):
                out = out + diag_t[w, 0:NVAR] * face_ref[u, w, k : k + 1]
            folded[k, u] = pad_rows(out)
    swap_start(*fold_swap())

    live = (iota((1, slots), 1) < count_ref[...]).astype(jnp.float32)
    cell_table[...] = jnp.where(iota((cells, slots), 0) == cell_ref[...], 1.0, 0.0).astype(
        jnp.bfloat16
    )
    for t in range(TMAP):
        node = node_ref[t : t + 1]
        block_of = lax.shift_right_logical(node, NPB.bit_length() - 1)
        inside = node & (NPB - 1)
        block_table[:, t * slots : (t + 1) * slots] = jnp.where(
            iota((shell_total, slots), 0) == block_of, 1.0, 0.0
        ).astype(jnp.bfloat16)
        node_mask[:, t * slots : (t + 1) * slots] = jnp.where(
            iota((NPB, slots), 0) == inside, weight_ref[t : t + 1], 0.0
        )
    for c in range(0, BLK * BLK, CHUNK):
        offset = iota((LANE, CHUNK), 1) + c - BLK * iota((LANE, CHUNK), 0)
        expand[:, c : c + CHUNK] = jnp.where((offset >= 0) & (offset < BLK), 1.0, 0.0).astype(
            jnp.bfloat16
        )
    out_row = iota((3 * NPB, LANE), 0)
    perm = jnp.where(
        iota((3 * NPB, LANE), 1)
        == (out_row & (NPB - 1)) * DOF + lax.shift_right_logical(out_row, NPB.bit_length() - 1),
        1.0,
        0.0,
    ).astype(jnp.bfloat16)
    behind = iota((FOLD, LANE), 0) - iota((FOLD, LANE), 1)
    near = (behind == 0) | (behind == BLK) | (behind == 2 * BLK) | (behind == 3 * BLK)
    fold = jnp.where(near & (iota((FOLD, LANE), 1) < BLK), 1.0, 0.0).astype(jnp.bfloat16)

    struct_all[pl.ds(pl.multiple_of(me_s * shard_rows, shard_rows), shard_rows)] = start_struct[...]
    for r in range(1, struct_n):
        source = (me_s + r) % struct_n
        copy = pltpu.make_async_remote_copy(
            src_ref=start_struct,
            dst_ref=struct_land.at[source],
            send_sem=start_send.at[r],
            recv_sem=start_recv.at[source],
            device_id=(me_f, source),
            device_id_type=MESH,
        )
        copy.wait()
        struct_all[pl.ds(pl.multiple_of(source * shard_rows, shard_rows), shard_rows)] = (
            struct_land[source]
        )

    def all_copies(iteration, sources, dest, send, recv, mode):
        def one(r, carry):
            peer = (me + r) % total
            peer_f, peer_s = dev(peer)
            if mode == "start":
                source = sources(peer_s * fluid_n + peer_f)
                landing = me
            else:
                source = sources(0)
                landing = peer
            copy = pltpu.make_async_remote_copy(
                src_ref=source,
                dst_ref=dest(landing),
                send_sem=send.at[iteration, r],
                recv_sem=recv.at[iteration, landing],
                device_id=(peer_f, peer_s),
                device_id_type=MESH,
            )
            if mode == "start":
                copy.start()
            else:
                copy.wait()
            return carry

        lax.fori_loop(1, total, one, 0)

    def shell_terms():
        for m in range(NB):
            for i in range(ROWS):
                column = columns_ref[m, base + i]
                rows_x[m * ROWS + i : m * ROWS + i + 1] = struct_all[pl.ds(column, 1)]
        if iteration == 0:
            for copy in local:
                copy.wait()
        entries = rows_x[...]
        parts = jnp.concatenate([p.astype(jnp.float32) for p in split(entries)], axis=0).astype(
            jnp.bfloat16
        )
        count = NB * ROWS
        acc = jnp.zeros((ROWS, FOLD), jnp.float32)
        for c in range(0, BLK * BLK, CHUNK):
            wide = dot(parts, expand[:, c : c + CHUNK], NN)
            wide = wide[0:count] + (wide[count : 2 * count] + wide[2 * count :])
            for m in range(NB):
                product = wide[m * ROWS : (m + 1) * ROWS] * blocks[m, :, c : c + CHUNK]
                for g in range(0, CHUNK, FOLD):
                    acc = acc + product[:, g : g + FOLD]
        terms[...] = dot_left(acc, fold, NN)

    width = 3 * NPB
    for iteration in range(ITERS):
        first = iteration * SWEEPS
        by_node = dot_right(perm, struct_all[...], NT)
        picked = dot_left(by_node, block_table[...], NN)
        moved = []
        for j in range(3):
            masked = picked[j * NPB : (j + 1) * NPB] * node_mask[...]
            shifted = masked[:, 0:slots]
            for t in range(1, TMAP):
                shifted = shifted + masked[:, t * slots : (t + 1) * slots]
            moved.append(jnp.sum(shifted, axis=0, keepdims=True))
        displaced = jnp.concatenate(moved, axis=0)
        coupled = jnp.concatenate(
            [jnp.sum(load_ref[v] * displaced, axis=0, keepdims=True) for v in range(NVAR)], axis=0
        )
        coupling = dot_left(pad_rows(coupled * live), cell_table[...], NT)
        right = coupling[0:NVAR] + rhs_ref[...]
        out = jnp.zeros((NVAR, cells), jnp.float32)
        for w in range(NVAR):
            out = out + diag_t[w, 0:NVAR] * right[w : w + 1]
        bias[iteration] = pad_rows(out)
        swap_start(*bias_swap(iteration))

        for sweep in range(SWEEPS):
            t = first + sweep
            if sweep == 1:
                shell_terms()
            wide = sweep in WIDE
            if sweep - 1 not in WIDE:
                swap_wait(*halo(t))
                whole = []
                for ref in (low_halo, state, high_halo):
                    for a in range(tiles):
                        whole.append(ref[t, :, a * LANE : (a + 1) * LANE])
            if iteration == 0 and sweep == WIDE[0]:
                swap_wait(*index_swap())
                swap_wait(*fold_swap())
            if sweep == WIDE[0]:
                swap_wait(*bias_swap(iteration))
            targets = [(folded, bias, index_all, a, tiles + a, tiles - half_tiles) for a in range(tiles)]
            if wide:
                for a in range(half_tiles):
                    targets.append(
                        (fold_low, bias_low, index_low, a, tiles - half_tiles + a, -half_tiles)
                    )
                    targets.append(
                        (fold_high, bias_high, index_high, a, 2 * tiles + a, 2 * tiles - half_tiles)
                    )
            after = [None] * (3 * tiles)
            for fold_ref, bias_ref, place_ref, a, at, shift in targets:
                span = slice(a * LANE, (a + 1) * LANE)
                acc = bias_ref[iteration, :, span]
                for k in range(FACES):
                    index = jnp.broadcast_to(place_ref[k : k + 1, span], (ROWS, LANE))
                    lane = index & (LANE - 1)
                    tile = lax.shift_right_logical(index, 7) + shift
                    beside = None
                    for b in range(at - half_tiles, at + half_tiles + 1):
                        found = jnp.take_along_axis(
                            whole[b], lane, axis=1, mode="promise_in_bounds"
                        )
                        beside = found if beside is None else jnp.where(tile == b, found, beside)
                    for u in range(NVAR):
                        acc = acc - fold_ref[k, u, :, span] * beside[u : u + 1]
                after[at] = acc
                if at == tiles + a:
                    state[t + 1, :, span] = acc
            whole = after
            if t + 1 < ITERS * SWEEPS and not wide:
                swap_start(*halo(t + 1))

        last = state[first + SWEEPS]
        at_surface = dot_left(last, cell_table[...], (((1,), (0,)), ((), ())))
        sens = jnp.zeros((3, slots), jnp.float32)
        for v in range(NVAR):
            sens = sens + disp_ref[v] * at_surface[v : v + 1]
        sens = sens * live
        scaled = []
        for j in range(3):
            row = sens[j : j + 1]
            scaled.append(node_mask[...] * jnp.concatenate([row] * TMAP, axis=1))
        values = jnp.concatenate(scaled, axis=0)
        forces = dot_right(block_table[...], values, NT)
        for p in range(total):
            forces_out[iteration, p, :, 0:width] = forces[p * piece : (p + 1) * piece]
        all_copies(
            iteration,
            lambda p: forces_out.at[iteration, p],
            lambda q: forces_land.at[iteration, q],
            force_send,
            force_recv,
            "start",
        )
        forces_land[iteration, me] = forces_out[iteration, me_s * fluid_n + me_f]
        all_copies(
            iteration,
            lambda p: forces_out.at[iteration, p],
            lambda q: forces_land.at[iteration, q],
            force_send,
            force_recv,
            "wait",
        )
        mine = forces_land[iteration, 0]
        for q in range(1, total):
            mine = mine + forces_land[iteration, q]
        mine = jnp.concatenate([mine] * (ROWS // piece), axis=0)
        spread = dot_left(mine[:, 0:width], perm, NN)
        load = right_struct[pl.ds(pl.multiple_of(base, ROWS), ROWS)] + spread - terms[...]
        tiled = dot_left(load, fold, NT)
        solved = jnp.zeros((3 * ROWS, LANE), jnp.float32)
        for c in range(0, BLK * BLK, CHUNK):
            product = inverse[:, c : c + CHUNK] * jnp.concatenate([tiled] * (CHUNK // FOLD), axis=1)
            parts = jnp.concatenate(
                [p.astype(jnp.float32) for p in split(product)], axis=0
            ).astype(jnp.bfloat16)
            solved = solved + dot(parts, expand[:, c : c + CHUNK], NT)
        solved = solved[0:ROWS] + (solved[ROWS : 2 * ROWS] + solved[2 * ROWS :])
        for g in range(ROWS // piece):
            @pl.when(my_row - base == g * piece)
            def _():
                result[iteration] = solved[g * piece : (g + 1) * piece]

        if iteration + 1 < ITERS:
            all_copies(
                iteration,
                lambda p: result.at[iteration],
                lambda q: final_land.at[iteration, q],
                gather_send,
                gather_recv,
                "start",
            )
            final_land[iteration, me] = result[iteration]
            all_copies(
                iteration,
                lambda p: result.at[iteration],
                lambda q: final_land.at[iteration, q],
                gather_send,
                gather_recv,
                "wait",
            )
            for q in range(total):
                f, s = q // struct_n, q % struct_n
                row = (s * fluid_n + f) * piece
                struct_all[row : row + piece] = final_land[iteration, q]
        else:
            def one(r, landing_f, action):
                copy = pltpu.make_async_remote_copy(
                    src_ref=result.at[iteration],
                    dst_ref=final_land.at[iteration, landing_f],
                    send_sem=gather_send.at[iteration, r],
                    recv_sem=gather_recv.at[iteration, landing_f],
                    device_id=((me_f + r) % fluid_n, me_s),
                    device_id_type=MESH,
                )
                getattr(copy, action)()

            for r in range(1, fluid_n):
                one(r, me_f, "start")
            fluid_ref[...] = last[0:NVAR]
            final_land[iteration, me_f] = result[iteration]
            for r in range(1, fluid_n):
                one(r, (me_f + r) % fluid_n, "wait")
            for f in range(fluid_n):
                struct_ref[f * piece : (f + 1) * piece] = final_land[iteration, f]


def body(
    fluid_n,
    struct_n,
    fluid_adjoint,
    fluid_rhs,
    diag_inverse,
    face_blocks,
    face_index,
    surface_cell,
    surface_count,
    transfer_node,
    transfer_weight,
    load_sens,
    disp_sens,
    struct_adjoint,
    struct_rhs,
    shell_blocks,
    shell_inverse,
    shell_columns,
):
    cells = fluid_adjoint.shape[1]
    slots = surface_cell.shape[0]
    block_rows = struct_adjoint.shape[0] // BLK
    shell_total = block_rows * struct_n
    piece = block_rows // fluid_n
    total = fluid_n * struct_n
    half = cells // 2
    sweeps = ITERS * SWEEPS
    vmem = pl.BlockSpec(memory_space=pltpu.VMEM)
    far = pl.BlockSpec(memory_space=pl.ANY)
    smem = pl.BlockSpec(memory_space=pltpu.SMEM)
    f32, bf16 = jnp.float32, jnp.bfloat16
    dma = pltpu.SemaphoreType.DMA

    fluid_out, struct_out = pl.pallas_call(
        functools.partial(kernel, fluid_n, struct_n, piece),
        out_shape=(
            jax.ShapeDtypeStruct((NVAR, cells), f32),
            jax.ShapeDtypeStruct((block_rows, LANE), f32),
        ),
        in_specs=[vmem] * 13 + [far, far, smem],
        out_specs=(vmem, vmem),
        scratch_shapes=[
            pltpu.VMEM((sweeps + 1, ROWS, cells), f32),
            pltpu.VMEM((sweeps, ROWS, cells), f32),
            pltpu.VMEM((sweeps, ROWS, cells), f32),
            pltpu.VMEM((FACES, NVAR, ROWS, cells), f32),
            pltpu.VMEM((FACES, NVAR, ROWS, half), f32),
            pltpu.VMEM((FACES, NVAR, ROWS, half), f32),
            pltpu.VMEM((ITERS, ROWS, cells), f32),
            pltpu.VMEM((ITERS, ROWS, half), f32),
            pltpu.VMEM((ITERS, ROWS, half), f32),
            pltpu.VMEM((ROWS, cells), jnp.int32),
            pltpu.VMEM((ROWS, half), jnp.int32),
            pltpu.VMEM((ROWS, half), jnp.int32),
            pltpu.VMEM((NVAR, ROWS, cells), f32),
            pltpu.VMEM((cells, slots), bf16),
            pltpu.VMEM((shell_total, TMAP * slots), bf16),
            pltpu.VMEM((NPB, TMAP * slots), f32),
            pltpu.VMEM((NB, ROWS, BLK * BLK), f32),
            pltpu.VMEM((ROWS, BLK * BLK), f32),
            pltpu.VMEM((LANE, BLK * BLK), bf16),
            pltpu.VMEM((block_rows, LANE), f32),
            pltpu.VMEM((block_rows, LANE), f32),
            pltpu.VMEM((struct_n, block_rows, LANE), f32),
            pltpu.VMEM((shell_total, LANE), f32),
            pltpu.VMEM((NB * ROWS, LANE), f32),
            pltpu.VMEM((ROWS, LANE), f32),
            pltpu.VMEM((ITERS, total, piece, LANE), f32),
            pltpu.VMEM((ITERS, total, piece, LANE), f32),
            pltpu.VMEM((ITERS, piece, LANE), f32),
            pltpu.VMEM((ITERS, total, piece, LANE), f32),
            dma((sweeps, 2)),
            dma((sweeps, 2)),
            dma((2 + ITERS, 2)),
            dma((2 + ITERS, 2)),
            dma((struct_n,)),
            dma((struct_n,)),
            dma((ITERS, total)),
            dma((ITERS, total)),
            dma((ITERS, total)),
            dma((ITERS, total)),
            dma((NB + 1,)),
        ],
        compiler_params=pltpu.CompilerParams(collective_id=0, has_side_effects=True),
    )(
        fluid_adjoint,
        fluid_rhs,
        diag_inverse,
        jnp.transpose(face_blocks, (1, 2, 0, 3)),
        face_index,
        surface_cell.reshape(1, slots),
        surface_count.reshape(1, 1),
        transfer_node,
        transfer_weight,
        jnp.transpose(load_sens, (1, 0, 2)),
        disp_sens,
        struct_adjoint.reshape(-1, LANE),
        struct_rhs.reshape(-1, LANE),
        shell_blocks,
        shell_inverse,
        shell_columns,
    )
    return fluid_out, struct_out[:, 0:BLK].reshape(-1)


def solution(mesh):
    placed = (
        P(None, ("fluid", "struct")),
        P(None, ("fluid", "struct")),
        P(None, None, ("fluid", "struct")),
        P(None, None, None, ("fluid", "struct")),
        P(None, ("fluid", "struct")),
        P(("fluid", "struct")),
        P(("fluid", "struct")),
        P(None, ("fluid", "struct")),
        P(None, ("fluid", "struct")),
        P(None, None, ("fluid", "struct")),
        P(None, None, ("fluid", "struct")),
        P("struct"),
        P("struct"),
        P(None, "struct", None),
        P("struct", None),
        P(None, "struct"),
    )
    return jax.shard_map(
        functools.partial(body, mesh.shape["fluid"], mesh.shape["struct"]),
        mesh=mesh,
        in_specs=placed,
        out_specs=(P(None, ("fluid", "struct")), P("struct")),
        check_vma=False,
    )
```

profile of v0, /device:TPU:0, one launch (start us, length us, event | category | flops | bytes accessed | tf_op | source)
XLA Modules:
  0.0 70.9 jit_solution(1367811281524576998)
XLA Ops:
  1.3 66.9 %shard_map.167 = (f32[5,512]{1,0:T(8,128)}, f32[32,128]{1,0:T(8,128)}) custom-call(f32[5,512]{1,0:T(8,128)} %adj_ref.1, f32[5,512]{1,0:T(8,128)} %rhs_ref.1, f32[5,5,512]{2,1,0:T(8,128)} %diag_ref.1, f32[5,5,6,512]{3,2,1,0:T(8,128)} %bitcast.8, s32[6,512]{1,0:T(8,128)} %index_ref.1, s32[1,256]{1,0:T(1,128)} %bitcast.13, s32[1,1]{1,0:T(1,128)} %bitcast.7.count_ref, ...), custom_call_target="tpu_custom_call" | custom-call | tf_op jit(solution)/shard_map/pallas_call | solution.py:592
  68.2 1.4 %reshape.23 = f32[3072]{0:T(1024)} reshape(f32[32,96]{1,0:T(8,128)} %bitcast.10) | data formatting | bytes 24576 | tf_op jit(solution)/shard_map/reshape | solution.py:661
  69.6 1.3 %copy.20 = f32[5,512]{1,0:T(8,128)} copy(f32[5,512]{1,0:T(8,128)} %get-tuple-element.8) | data formatting | bytes 20480
where the time goes:
time: 71.3 us; the launch traced here: 70.9 us
  Pallas kernels  66.9 us (94%)
  local copies, waits for them, and re-layouts  2.71 us (4%)
  between operations  1.29 us (2%)
    pallas_call x1, Pallas kernels, body(): pl.pallas_call(functools.partial(kernel, fluid_n, struct_n, piece), out_s...  66.9 us

commit v1 on v0

--- a/solution.py
+++ b/solution.py
@@ -28,10 +28,7 @@
 
 def split(value):
     high = value.astype(jnp.bfloat16)
-    rest = value - high.astype(jnp.float32)
-    middle = rest.astype(jnp.bfloat16)
-    low = (rest - middle.astype(jnp.float32)).astype(jnp.bfloat16)
-    return high, middle, low
+    return high, (value - high.astype(jnp.float32)).astype(jnp.bfloat16)
 
 
 def dot(left, right, dims):
@@ -42,12 +39,12 @@
     rows = value.shape[0]
     stacked = jnp.concatenate([p.astype(jnp.float32) for p in split(value)], axis=0)
     out = dot(stacked.astype(jnp.bfloat16), table, dims)
-    return out[0:rows] + (out[rows : 2 * rows] + out[2 * rows : 3 * rows])
+    return out[0:rows] + out[rows : 2 * rows]
 
 
 def dot_right(table, value, dims):
-    high, middle, low = split(value)
-    return dot(table, high, dims) + (dot(table, middle, dims) + dot(table, low, dims))
+    high, low = split(value)
+    return dot(table, high, dims) + dot(table, low, dims)
 
 
 def iota(shape, axis):
@@ -132,6 +129,8 @@
     force_recv,
     gather_send,
     gather_recv,
+    final_send,
+    final_recv,
     local_sem,
 ):
     me_f = lax.axis_index("fluid")
@@ -339,31 +338,36 @@
             struct_land[source]
         )
 
+    peers_f = [(me_f + r) % fluid_n for r in range(fluid_n)]
+    peers_s = [(me_s + r) % struct_n for r in range(struct_n)]
+
     def all_copies(iteration, sources, dest, send, recv, mode):
-        def one(r, carry):
-            peer = (me + r) % total
-            peer_f, peer_s = dev(peer)
-            if mode == "start":
-                source = sources(peer_s * fluid_n + peer_f)
-                landing = me
-            else:
-                source = sources(0)
-                landing = peer
-            copy = pltpu.make_async_remote_copy(
-                src_ref=source,
-                dst_ref=dest(landing),
-                send_sem=send.at[iteration, r],
-                recv_sem=recv.at[iteration, landing],
-                device_id=(peer_f, peer_s),
+        if mode == "start":
+            for rf in reversed(range(fluid_n)):
+                for rs in reversed(range(struct_n)):
+                    if rf + rs == 0:
+                        continue
+                    peer_f, peer_s = peers_f[rf], peers_s[rs]
+                    pltpu.make_async_remote_copy(
+                        src_ref=sources(peer_s * fluid_n + peer_f),
+                        dst_ref=dest(me),
+                        send_sem=send.at[iteration],
+                        recv_sem=recv.at[iteration],
+                        device_id=(peer_f, peer_s),
+                        device_id_type=MESH,
+                    ).start()
+        else:
+            every = dest(slice(0, total - 1))
+            done = pltpu.make_async_remote_copy(
+                src_ref=every,
+                dst_ref=every,
+                send_sem=send.at[iteration],
+                recv_sem=recv.at[iteration],
+                device_id=(peers_f[1], me_s),
                 device_id_type=MESH,
             )
-            if mode == "start":
-                copy.start()
-            else:
-                copy.wait()
-            return carry
-
-        lax.fori_loop(1, total, one, 0)
+            done.wait_recv()
+            done.wait_send()
 
     def shell_terms():
         for m in range(NB):
@@ -381,7 +385,7 @@
         acc = jnp.zeros((ROWS, FOLD), jnp.float32)
         for c in range(0, BLK * BLK, CHUNK):
             wide = dot(parts, expand[:, c : c + CHUNK], NN)
-            wide = wide[0:count] + (wide[count : 2 * count] + wide[2 * count :])
+            wide = wide[0:count] + wide[count:]
             for m in range(NB):
                 product = wide[m * ROWS : (m + 1) * ROWS] * blocks[m, :, c : c + CHUNK]
                 for g in range(0, CHUNK, FOLD):
@@ -498,14 +502,14 @@
         spread = dot_left(mine[:, 0:width], perm, NN)
         load = right_struct[pl.ds(pl.multiple_of(base, ROWS), ROWS)] + spread - terms[...]
         tiled = dot_left(load, fold, NT)
-        solved = jnp.zeros((3 * ROWS, LANE), jnp.float32)
+        solved = jnp.zeros((2 * ROWS, LANE), jnp.float32)
         for c in range(0, BLK * BLK, CHUNK):
             product = inverse[:, c : c + CHUNK] * jnp.concatenate([tiled] * (CHUNK // FOLD), axis=1)
             parts = jnp.concatenate(
                 [p.astype(jnp.float32) for p in split(product)], axis=0
             ).astype(jnp.bfloat16)
             solved = solved + dot(parts, expand[:, c : c + CHUNK], NT)
-        solved = solved[0:ROWS] + (solved[ROWS : 2 * ROWS] + solved[2 * ROWS :])
+        solved = solved[0:ROWS] + solved[ROWS:]
         for g in range(ROWS // piece):
             @pl.when(my_row - base == g * piece)
             def _():
@@ -538,8 +542,8 @@
                 copy = pltpu.make_async_remote_copy(
                     src_ref=result.at[iteration],
                     dst_ref=final_land.at[iteration, landing_f],
-                    send_sem=gather_send.at[iteration, r],
-                    recv_sem=gather_recv.at[iteration, landing_f],
+                    send_sem=final_send.at[r],
+                    recv_sem=final_recv.at[landing_f],
                     device_id=((me_f + r) % fluid_n, me_s),
                     device_id_type=MESH,
                 )
@@ -553,6 +557,17 @@
                 one(r, (me_f + r) % fluid_n, "wait")
             for f in range(fluid_n):
                 struct_ref[f * piece : (f + 1) * piece] = final_land[iteration, f]
+
+
+def finish(fluid_in, struct_in, fluid_ref, struct_ref):
+    fluid_ref[...] = fluid_in[...]
+    per = FOLD // BLK
+    groups = struct_in.shape[0] // per
+    wide = jnp.concatenate(
+        [struct_in[pl.ds(q, groups, stride=per)][:, 0:BLK] for q in range(per)], axis=1
+    )
+    for q in range(FOLD // LANE):
+        struct_ref[pl.ds(q, groups, stride=FOLD // LANE)] = wide[:, q * LANE : (q + 1) * LANE]
 
 
 def body(
@@ -633,10 +648,12 @@
             dma((2 + ITERS, 2)),
             dma((struct_n,)),
             dma((struct_n,)),
-            dma((ITERS, total)),
-            dma((ITERS, total)),
-            dma((ITERS, total)),
-            dma((ITERS, total)),
+            dma((ITERS,)),
+            dma((ITERS,)),
+            dma((ITERS,)),
+            dma((ITERS,)),
+            dma((fluid_n,)),
+            dma((fluid_n,)),
             dma((NB + 1,)),
         ],
         compiler_params=pltpu.CompilerParams(collective_id=0, has_side_effects=True),
@@ -658,7 +675,16 @@
         shell_inverse,
         shell_columns,
     )
-    return fluid_out, struct_out[:, 0:BLK].reshape(-1)
+    fluid_out, struct_out = pl.pallas_call(
+        finish,
+        out_shape=(
+            jax.ShapeDtypeStruct((NVAR, cells), f32),
+            jax.ShapeDtypeStruct((block_rows * BLK // LANE, LANE), f32),
+        ),
+        in_specs=[vmem, vmem],
+        out_specs=(vmem, vmem),
+    )(fluid_out, struct_out)
+    return fluid_out, struct_out.reshape(-1)
 
 
 def solution(mesh):

time: 71.3 us -> 66.4 us (0.931)
  local copies, waits for them, and re-layouts: 2.71 us -> 0 us
  Pallas kernels: 66.9 us -> 64.8 us
    pallas_call x1, Pallas kernels: 66.9 us -> 63.4 us  [body(): pl.pallas_call(functools.partial(kernel, fluid_n, struct_n, piece), out_s...]
    pallas_call x0 -> x1, Pallas kernels: none -> 1.41 us  [body(): pl.pallas_call(finish, out_shape=(jax.ShapeDtypeStruct((NVAR, cells), f32...]
    reshape x1 -> x0, local copies, waits for them, and re-layouts: 1.39 us -> none  [body(): return (fluid_out, struct_out[:, 0:BLK].reshape(-1))]
    unnamed x1 -> x0, local copies, waits for them, and re-layouts: 1.32 us -> none
where the time goes in v1:
time: 66.4 us; the launch traced here: 66.1 us
  Pallas kernels  64.8 us (98%)
  between operations  1.29 us (2%)
    pallas_call x1, Pallas kernels, body(): pl.pallas_call(functools.partial(kernel, fluid_n, struct_n, piece), out_s...  63.4 us
    pallas_call x1, Pallas kernels, body(): pl.pallas_call(finish, out_shape=(jax.ShapeDtypeStruct((NVAR, cells), f32...  1.41 us

profile of v1, /device:TPU:0, one launch (start us, length us, event | category | flops | bytes accessed | tf_op | source)
XLA Modules:
  0.0 66.1 jit_solution(13314523308453046629)
XLA Ops:
  1.3 63.4 %shard_map.167 = (f32[5,512]{1,0:T(8,128)}, f32[32,128]{1,0:T(8,128)}) custom-call(f32[5,512]{1,0:T(8,128)} %adj_ref.1, f32[5,512]{1,0:T(8,128)} %rhs_ref.1, f32[5,5,512]{2,1,0:T(8,128)} %diag_ref.1, f32[5,5,6,512]{3,2,1,0:T(8,128)} %bitcast.8, s32[6,512]{1,0:T(8,128)} %index_ref.1, s32[1,256]{1,0:T(1,128)} %bitcast.12, s32[1,1]{1,0:T(1,128)} %bitcast.7.count_ref, ...), custom_call_target="tpu_custom_call" | custom-call | tf_op jit(solution)/shard_map/pallas_call | solution.py:607
  64.7 1.4 %shard_map.168 = (f32[5,512]{1,0:T(8,128)}, f32[24,128]{1,0:T(8,128)}) custom-call(f32[5,512]{1,0:T(8,128)} %get-tuple-element.6.fluid_in, f32[32,128]{1,0:T(8,128)} %get-tuple-element.7.struct_in), custom_call_target="tpu_custom_call" | custom-call | tf_op jit(solution)/shard_map/pallas_call | solution.py:678

commit v2 on v1

v2 whole, which is shorter than its diff:
```python
import functools

import jax
import jax.numpy as jnp
from jax import lax
from jax.experimental import pallas as pl
from jax.experimental.pallas import tpu as pltpu
from jax.sharding import PartitionSpec as P

NVAR = 5
FACES = 6
TMAP = 3
DOF = 6
BLK = 96
NB = 4
SWEEPS = 6
ITERS = 2
NPB = BLK // DOF
LANE = 128
ROWS = 8
FOLD = 384
CHUNK = 768
NEAR = (2, 5)
FAR = 3
MESH = pl.DeviceIdType.MESH
NN = (((1,), (0,)), ((), ()))
NT = (((1,), (1,)), ((), ()))


def split(value):
    high = value.astype(jnp.bfloat16)
    return high, (value - high.astype(jnp.float32)).astype(jnp.bfloat16)


def dot(left, right, dims):
    return lax.dot_general(left, right, dims, preferred_element_type=jnp.float32)


def dot_left(value, table, dims):
    rows = value.shape[0]
    stacked = jnp.concatenate([p.astype(jnp.float32) for p in split(value)], axis=0)
    out = dot(stacked.astype(jnp.bfloat16), table, dims)
    return out[0:rows] + out[rows : 2 * rows]


def dot_right(table, value, dims):
    high, low = split(value)
    return dot(table, high, dims) + dot(table, low, dims)


def iota(shape, axis):
    return lax.broadcasted_iota(jnp.int32, shape, axis)


def pad_rows(value, rows=ROWS):
    return jnp.concatenate(
        [value, jnp.zeros((rows - value.shape[0], value.shape[1]), value.dtype)], axis=0
    )


def by_block(flat, out):
    groups = flat.shape[0] * LANE // FOLD
    wide = jnp.concatenate(
        [flat[pl.ds(a, groups, stride=FOLD // LANE)] for a in range(FOLD // LANE)], axis=1
    )
    for q in range(FOLD // BLK):
        part = wide[:, q * BLK : (q + 1) * BLK]
        full = jnp.concatenate([part, jnp.zeros((groups, LANE - BLK), jnp.float32)], axis=1)
        out[pl.ds(q, groups, stride=FOLD // BLK)] = full


def kernel(
    fluid_n,
    struct_n,
    piece,
    adj_far,
    rhs_far,
    diag_far,
    face_far,
    index_far,
    cell_far,
    count_ref,
    node_far,
    weight_far,
    load_far,
    disp_far,
    sadj_far,
    srhs_far,
    blocks_ref,
    inverse_ref,
    columns_far,
    fluid_ref,
    struct_ref,
    state,
    work,
    folded,
    code,
    pair_fold,
    pair_code,
    base_bias,
    bias,
    partial,
    mix,
    mix_int,
    fold_mix,
    diag_mix,
    pack,
    pack_near,
    cell_table,
    block_table,
    node_mask,
    blocks,
    inverse,
    expand,
    start_struct,
    right_struct,
    struct_all,
    rows_x,
    terms,
    forces_out,
    forces_land,
    result,
    final_land,
    state_send,
    state_recv,
    once_send,
    once_recv,
    start_send,
    start_recv,
    force_send,
    force_recv,
    gather_send,
    gather_recv,
    final_send,
    final_recv,
    local_sem,
    input_sem,
    adj_ref,
    rhs_ref,
    diag_ref,
    face_ref,
    index_ref,
    cell_ref,
    node_ref,
    weight_ref,
    load_ref,
    disp_ref,
    sadj_ref,
    srhs_ref,
    columns_ref,
):
    me_f = lax.axis_index("fluid")
    me_s = lax.axis_index("struct")
    me = me_f * struct_n + me_s
    total = fluid_n * struct_n
    cells = adj_ref.shape[1]
    tiles = cells // LANE
    half = tiles // 2
    slots = cell_ref.shape[1]
    shell_total = struct_all.shape[1]
    shard_rows = start_struct.shape[0]
    my_row = me_f * piece
    base = (my_row // ROWS) * ROWS
    own_row = me_s * shard_rows + my_row
    own_x = 3 * half
    own = tiles

    def dev(index):
        return (index // struct_n, index % struct_n)

    peers_f = [(me_f + r) % fluid_n for r in range(fluid_n)]
    peers_s = [(me_s + r) % struct_n for r in range(struct_n)]
    barrier = pltpu.get_barrier_semaphore()
    for rf in reversed(range(fluid_n)):
        for rs in reversed(range(struct_n)):
            if rf + rs:
                pl.semaphore_signal(
                    barrier, inc=1, device_id=(peers_f[rf], peers_s[rs]), device_id_type=MESH
                )

    inputs = []
    for n, (source, landing) in enumerate(
        (
            (sadj_far, sadj_ref),
            (adj_far, adj_ref),
            (srhs_far, srhs_ref),
            (diag_far, diag_ref),
            (face_far, face_ref),
            (index_far, index_ref),
            (cell_far, cell_ref),
            (node_far, node_ref),
            (weight_far, weight_ref),
            (load_far, load_ref),
            (rhs_far, rhs_ref),
            (disp_far, disp_ref),
            (columns_far, columns_ref),
        )
    ):
        inputs.append(pltpu.make_async_copy(source, landing, input_sem.at[n]))
        inputs[n].start()
    local = []
    for m in range(NB):
        local.append(
            pltpu.make_async_copy(
                blocks_ref.at[m, pl.ds(pl.multiple_of(base, ROWS), ROWS)],
                blocks.at[m],
                local_sem.at[m],
            )
        )
    local.append(
        pltpu.make_async_copy(
            inverse_ref.at[pl.ds(pl.multiple_of(base, ROWS), ROWS)], inverse, local_sem.at[NB]
        )
    )
    for copy in local:
        copy.start()

    shifts = (-1, 1, -2, 2)
    sends = (me > 0, me < total - 1, me > 1, me < total - 2)
    takes = (me < total - 1, me > 0, me < total - 2, me > 1)

    def swap_start(copies, send, recv):
        for d, (source, landing) in enumerate(copies):
            @pl.when(sends[d])
            def _():
                pltpu.make_async_remote_copy(
                    src_ref=source,
                    dst_ref=landing,
                    send_sem=send.at[d],
                    recv_sem=recv.at[d],
                    device_id=dev(me + shifts[d]),
                    device_id_type=MESH,
                ).start()

    def swap_wait(copies, send, recv):
        for d, (source, landing) in enumerate(copies):
            copy = pltpu.make_async_remote_copy(
                src_ref=source,
                dst_ref=landing,
                send_sem=send.at[d],
                recv_sem=recv.at[d],
                device_id=dev(me + shifts[d]),
                device_id_type=MESH,
            )

            @pl.when(takes[d])
            def _():
                copy.wait_recv()

            @pl.when(sends[d])
            def _():
                copy.wait_send()

    def rows(ref, first, count):
        return ref.at[:, first : first + count]

    def state_swap(e, wide):
        now = state.at[e]
        copies = [
            (rows(now, own_x, tiles), rows(now, own_x + tiles, tiles)),
            (rows(now, own_x, tiles), rows(now, own_x - tiles, tiles)),
        ]
        if wide:
            copies += [
                (rows(now, own_x, half), rows(now, own_x + 2 * tiles, half)),
                (rows(now, own_x + half, half), rows(now, 0, half)),
            ]
        return copies, state_send.at[e], state_recv.at[e]

    def row_swap(ref, n):
        copies = [
            (rows(ref, own, tiles), rows(ref, own + tiles, tiles)),
            (rows(ref, own, tiles), rows(ref, 0, tiles)),
        ]
        return copies, once_send.at[n], once_recv.at[n]

    def fold_swap(n, first_face, faces, far):
        some = folded.at[first_face * NVAR * NVAR : (first_face + faces) * NVAR * NVAR]
        low, high = rows(some, own, half), rows(some, own + half, half)
        if far:
            copies = [(high, rows(some, own + tiles + half, half)), (low, rows(some, 0, half))]
        else:
            copies = [(low, rows(some, own + tiles, half)), (high, rows(some, half, half))]
        return copies, once_send.at[n], once_recv.at[n]

    near_first = (0, 0, NEAR[0], False)
    near_next = (3, NEAR[0], NEAR[1] - NEAR[0], False)
    near_rest = (8, NEAR[1], FACES - NEAR[1], False)
    far_first = (6, 0, FAR, True)
    far_rest = (7, FAR, FACES - FAR, True)

    def pack_swap(n):
        copies = [(pack, pack_near.at[1]), (pack, pack_near.at[0])]
        return copies, once_send.at[n], once_recv.at[n]

    def span(a):
        return slice(a * LANE, (a + 1) * LANE)

    def to_rows(value, scratch, count):
        for a in range(tiles):
            scratch[a * ROWS : a * ROWS + count] = value[:, span(a)]
        return [scratch[pl.ds(v, tiles, stride=ROWS)] for v in range(count)]

    def clear(ref, first, count):
        ref[:, first : first + count] = jnp.zeros((ref.shape[0], count, LANE), ref.dtype)

    spare = state.shape[2]
    for e in range(state.shape[0]):
        clear(state.at[e], own_x + 2 * tiles + half, spare - own_x - 2 * tiles - half)

        @pl.when(me == 0)
        def _():
            clear(state.at[e], 0, own_x)

        @pl.when(me == 1)
        def _():
            clear(state.at[e], 0, half)

        @pl.when(me == total - 2)
        def _():
            clear(state.at[e], own_x + 2 * tiles, half)

        @pl.when(me == total - 1)
        def _():
            clear(state.at[e], own_x + tiles, tiles + half)

    @pl.when(me == 0)
    def _():
        for ref in (folded, code, base_bias, bias.at[0]):
            clear(ref, 0, tiles)
        pack_near[0] = jnp.zeros_like(pack)

    @pl.when(me == total - 1)
    def _():
        for ref in (folded, code, base_bias, bias.at[0]):
            clear(ref, own + tiles, tiles)
        pack_near[1] = jnp.zeros_like(pack)

    for copy in inputs[0:3]:
        copy.wait()
    for v, value in enumerate(to_rows(adj_ref[...], mix, NVAR)):
        state[0, v, own_x : own_x + tiles] = value
    by_block(sadj_ref, start_struct)
    by_block(srhs_ref, right_struct)
    forces_out[...] = jnp.zeros_like(forces_out)

    pl.semaphore_wait(barrier, total - 1)

    def start_copy(r, landing):
        return pltpu.make_async_remote_copy(
            src_ref=start_struct,
            dst_ref=struct_all.at[0, pl.ds(pl.multiple_of(landing * shard_rows, shard_rows), shard_rows)],
            send_sem=start_send.at[r],
            recv_sem=start_recv.at[landing],
            device_id=(me_f, peers_s[r]),
            device_id_type=MESH,
        )

    for r in range(1, struct_n):
        start_copy(r, me_s).start()
    swap_start(*state_swap(0, False))

    for copy in inputs[3:]:
        copy.wait()

    def pair(k):
        return slice((k % 2) * tiles, (k % 2 + 1) * tiles)

    for a in range(tiles):
        for v in range(NVAR):
            scale = [
                jnp.broadcast_to(diag_ref[v, w : w + 1, span(a)], (FACES, LANE)) for w in range(NVAR)
            ]
            for u in range(NVAR):
                out = scale[0] * face_ref[u, 0, :, span(a)]
                for w in range(1, NVAR):
                    out = out + scale[w] * face_ref[u, w, :, span(a)]
                at = ((u * NVAR + v) * tiles + a) * ROWS
                fold_mix[at : at + FACES] = out
    for k in range(FACES):
        for u in range(NVAR):
            for v in range(NVAR):
                at = (u * NVAR + v) * tiles * ROWS + k
                value = fold_mix[pl.ds(at, tiles, stride=ROWS)]
                folded[(k * NVAR + u) * NVAR + v, own : own + tiles] = value
                pair_fold[((k // 2) * NVAR + u) * NVAR + v, pair(k)] = value
        if k + 1 == NEAR[0]:
            swap_start(*fold_swap(*near_first))
    for k, value in enumerate(to_rows(index_ref[...], mix_int, FACES)):
        value = value - LANE * iota((tiles, LANE), 0)
        code[k, own : own + tiles] = value
        pair_code[k // 2, pair(k)] = value
    swap_start(*row_swap(code, 1))

    def tables(b, node_of, weight_of, cell_of):
        cell_table[b] = jnp.where(iota((cells, slots), 0) == cell_of, 1.0, 0.0).astype(jnp.bfloat16)
        for t in range(TMAP):
            node = node_of(t)
            block_of = lax.shift_right_logical(node, NPB.bit_length() - 1)
            inside = node & (NPB - 1)
            block_table[b, :, t * slots : (t + 1) * slots] = jnp.where(
                iota((shell_total, slots), 0) == block_of, 1.0, 0.0
            ).astype(jnp.bfloat16)
            node_mask[b, :, t * slots : (t + 1) * slots] = jnp.where(
                iota((NPB, slots), 0) == inside, weight_of(t), 0.0
            )

    live = (iota((1, slots), 1) < count_ref[...]).astype(jnp.float32)
    tables(0, lambda t: node_ref[t : t + 1], lambda t: weight_ref[t : t + 1], cell_ref[...])

    for u in range(NVAR):
        for v in range(NVAR):
            diag_mix[u * ROWS + v : u * ROWS + v + 1] = diag_ref[v, u : u + 1]
    at_slots = dot_left(diag_mix[...], cell_table[0], NN)
    for j in range(3):
        out = at_slots[0:NVAR] * load_ref[0, j : j + 1]
        for u in range(1, NVAR):
            out = out + at_slots[u * ROWS : u * ROWS + NVAR] * load_ref[u, j : j + 1]
        pack[j * ROWS : j * ROWS + NVAR] = out * live
    pack[NVAR : NVAR + TMAP] = weight_ref[...]
    pack[ROWS + NVAR : ROWS + NVAR + TMAP] = node_ref[...].astype(jnp.float32)
    pack[2 * ROWS + NVAR : 3 * ROWS] = jnp.concatenate(
        [cell_ref[...].astype(jnp.float32)] * (ROWS - NVAR), axis=0
    )

    for v in range(NVAR):
        mixed = jnp.sum(diag_ref[v] * rhs_ref[...], axis=0, keepdims=True)
        for a in range(tiles):
            base_bias[v, own + a : own + a + 1] = mixed[:, span(a)]

    for c in range(0, BLK * BLK, CHUNK):
        offset = iota((LANE, CHUNK), 1) + c - BLK * iota((LANE, CHUNK), 0)
        expand[:, c : c + CHUNK] = jnp.where((offset >= 0) & (offset < BLK), 1.0, 0.0).astype(
            jnp.bfloat16
        )
    width = 3 * NPB
    out_row = iota((width, LANE), 0)
    perm = jnp.where(
        iota((width, LANE), 1)
        == (out_row & (NPB - 1)) * DOF + lax.shift_right_logical(out_row, NPB.bit_length() - 1),
        1.0,
        0.0,
    ).astype(jnp.bfloat16)
    perm_twice = jnp.concatenate([perm, perm], axis=0)
    behind = iota((FOLD, LANE), 0) - iota((FOLD, LANE), 1)
    near = (behind == 0) | (behind == BLK) | (behind == 2 * BLK) | (behind == 3 * BLK)
    fold = jnp.where(near & (iota((FOLD, LANE), 1) < BLK), 1.0, 0.0).astype(jnp.bfloat16)

    def sweep(source, first, start):
        acc = list(start)
        for k in range(FACES):
            place = code[k, first : first + ROWS]
            lane = place & (LANE - 1)
            tile = lax.shift_right_logical(place, LANE.bit_length() - 1)
            picks = [tile == o for o in range(tiles + 1)]
            for u in range(NVAR):
                beside = None
                for o in range(tiles + 1):
                    found = jnp.take_along_axis(
                        source[u, first + o : first + o + ROWS], lane, axis=1, mode="promise_in_bounds"
                    )
                    beside = found if beside is None else jnp.where(picks[o], found, beside)
                for v in range(NVAR):
                    at = (k * NVAR + u) * NVAR + v
                    acc[v] = acc[v] - folded[at, first : first + ROWS] * beside
        return acc

    def own_sweep(source):
        acc = [None] * NVAR
        beside_rows = {}
        for u in range(NVAR):
            for o in range(tiles + 1):
                first = own_x - half + o
                once = source[u, first : first + tiles]
                beside_rows[u, o] = jnp.concatenate([once, once], axis=0)
        for k in range(FACES // 2):
            place = pair_code[k]
            lane = place & (LANE - 1)
            tile = lax.shift_right_logical(place, LANE.bit_length() - 1)
            picks = [tile == o for o in range(tiles + 1)]
            for u in range(NVAR):
                beside = None
                for o in range(tiles + 1):
                    found = jnp.take_along_axis(
                        beside_rows[u, o], lane, axis=1, mode="promise_in_bounds"
                    )
                    beside = found if beside is None else jnp.where(picks[o], found, beside)
                for v in range(NVAR):
                    term = pair_fold[(k * NVAR + u) * NVAR + v] * beside
                    acc[v] = term if acc[v] is None else acc[v] + term
        return [a[0:tiles] + a[tiles : 2 * tiles] for a in acc]

    def own_step(i, e, source):
        for v, taken in enumerate(own_sweep(source)):
            state[e, v, own_x : own_x + tiles] = bias[i, v, own : own + tiles] - taken

    def bias_rows(i, first):
        return [bias[i, v, first : first + ROWS] for v in range(NVAR)]

    def into_work(first, values):
        for v in range(NVAR):
            work[v, first + half : first + half + ROWS] = values[v]

    def last_steps(i, e):
        into_work(half, sweep(work, half, bias_rows(i, half)))
        own_step(i, e, work)

    def two_steps(i, e):
        into_work(half, sweep(state.at[e], half, bias_rows(i, half)))
        own_step(i, e + 1, work)

    def three_steps(i, e):
        outer = [sweep(state.at[e], f, bias_rows(i, f)) for f in (0, ROWS)]
        into_work(0, outer[0])
        into_work(ROWS, outer[1])
        last_steps(i, e + 1)

    def couple(i, which):
        by_node = dot_right(perm, struct_all[i], NT)
        parts = jnp.concatenate([p.astype(jnp.float32) for p in split(by_node)], axis=0).astype(
            jnp.bfloat16
        )
        for b in which:
            picked = dot(parts, block_table[b], NN)
            picked = picked[0:width] + picked[width : 2 * width]
            moved = []
            for j in range(3):
                masked = picked[j * NPB : (j + 1) * NPB] * node_mask[b]
                shifted = masked[:, 0:slots]
                for t in range(1, TMAP):
                    shifted = shifted + masked[:, t * slots : (t + 1) * slots]
                moved.append(jnp.sum(shifted, axis=0, keepdims=True))
            displaced = jnp.concatenate(moved, axis=0)
            rates = pack if b == 0 else pack_near.at[b - 1]
            coupled = rates[0:ROWS] * displaced[0:1]
            for j in range(1, 3):
                coupled = coupled + rates[j * ROWS : (j + 1) * ROWS] * displaced[j : j + 1]
            spread = dot_left(coupled, cell_table[b], NT)
            first = (own, 0, own + tiles)[b]
            for v, value in enumerate(to_rows(spread[0:NVAR], mix, NVAR)):
                bias[i, v, first : first + tiles] = base_bias[v, first : first + tiles] + value

    def all_start(source, landing, send, recv):
        for rf in reversed(range(fluid_n)):
            for rs in reversed(range(struct_n)):
                if rf + rs == 0:
                    continue
                peer_f, peer_s = peers_f[rf], peers_s[rs]
                pltpu.make_async_remote_copy(
                    src_ref=source(peer_s * fluid_n + peer_f),
                    dst_ref=landing,
                    send_sem=send,
                    recv_sem=recv,
                    device_id=(peer_f, peer_s),
                    device_id_type=MESH,
                ).start()

    def all_wait(every, send, recv):
        done = pltpu.make_async_remote_copy(
            src_ref=every,
            dst_ref=every,
            send_sem=send,
            recv_sem=recv,
            device_id=(peers_f[1], me_s),
            device_id_type=MESH,
        )
        done.wait_recv()
        done.wait_send()

    def shell_terms(i):
        for m in range(NB):
            for r in range(ROWS):
                column = columns_ref[m, base + r]
                rows_x[m * ROWS + r : m * ROWS + r + 1] = struct_all[i, pl.ds(column, 1)]
        if i == 0:
            for copy in local:
                copy.wait()
        entries = rows_x[...]
        parts = jnp.concatenate([p.astype(jnp.float32) for p in split(entries)], axis=0).astype(
            jnp.bfloat16
        )
        count = NB * ROWS
        acc = jnp.zeros((ROWS, FOLD), jnp.float32)
        for c in range(0, BLK * BLK, CHUNK):
            wide = dot(parts, expand[:, c : c + CHUNK], NN)
            wide = wide[0:count] + wide[count:]
            for m in range(NB):
                product = wide[m * ROWS : (m + 1) * ROWS] * blocks[m, :, c : c + CHUNK]
                for g in range(0, CHUNK, FOLD):
                    acc = acc + product[:, g : g + FOLD]
        terms[...] = dot_left(acc, fold, NN)

    def send_forces(i, e):
        for v in range(NVAR):
            mix[v * tiles : (v + 1) * tiles] = state[e, v, own_x : own_x + tiles]
        last = jnp.concatenate(
            [mix[pl.ds(a, NVAR, stride=tiles)] for a in range(tiles)], axis=1
        )
        at_surface = dot_left(pad_rows(last), cell_table[0], NN)
        sens = jnp.zeros((3, slots), jnp.float32)
        for v in range(NVAR):
            sens = sens + disp_ref[v] * at_surface[v : v + 1]
        sens = sens * live
        scaled = []
        for j in range(3):
            row = sens[j : j + 1]
            scaled.append(node_mask[0] * jnp.concatenate([row] * TMAP, axis=1))
        values = jnp.concatenate(scaled, axis=0)
        both = jnp.concatenate([p.astype(jnp.float32) for p in split(values)], axis=0)
        forces_out[i, :, 0 : 2 * width] = dot(block_table[0], both.astype(jnp.bfloat16), NT)
        all_start(
            lambda p: forces_out.at[i, pl.ds(pl.multiple_of(p * piece, piece), piece)],
            forces_land.at[i, me],
            force_send.at[i],
            force_recv.at[i],
        )
        forces_land[i, me] = forces_out[i, pl.ds(pl.multiple_of(own_row, piece), piece)]
        return last

    def solve(i):
        all_wait(forces_land.at[i, 0 : total - 1], force_send.at[i], force_recv.at[i])
        mine = forces_land[i, 0]
        for q in range(1, total):
            mine = mine + forces_land[i, q]
        mine = jnp.concatenate([mine] * (ROWS // piece), axis=0)
        spread = dot_left(mine[:, 0 : 2 * width], perm_twice, NN)
        load = right_struct[pl.ds(pl.multiple_of(base, ROWS), ROWS)] + spread - terms[...]
        tiled = dot_left(load, fold, NT)
        solved = jnp.zeros((2 * ROWS, LANE), jnp.float32)
        for c in range(0, BLK * BLK, CHUNK):
            product = inverse[:, c : c + CHUNK] * jnp.concatenate([tiled] * (CHUNK // FOLD), axis=1)
            parts = jnp.concatenate(
                [p.astype(jnp.float32) for p in split(product)], axis=0
            ).astype(jnp.bfloat16)
            solved = solved + dot(parts, expand[:, c : c + CHUNK], NT)
        solved = solved[0:ROWS] + solved[ROWS:]
        for g in range(ROWS // piece):
            @pl.when(my_row - base == g * piece)
            def _():
                result[i] = solved[g * piece : (g + 1) * piece]

    swap_wait(*state_swap(0, False))
    early = own_sweep(state.at[0])
    struct_all[0, pl.ds(pl.multiple_of(me_s * shard_rows, shard_rows), shard_rows)] = start_struct[...]
    for r in range(1, struct_n):
        start_copy(r, peers_s[r]).wait()
    couple(0, (0,))
    for v in range(NVAR):
        state[1, v, own_x : own_x + tiles] = bias[0, v, own : own + tiles] - early[v]
    swap_start(*state_swap(1, False))
    swap_start(*row_swap(bias.at[0], 2))
    swap_start(*fold_swap(*near_next))
    shell_terms(0)
    swap_wait(*state_swap(1, False))
    own_step(0, 2, state.at[1])
    swap_start(*state_swap(2, False))
    swap_start(*fold_swap(*near_rest))
    swap_start(*pack_swap(4))
    swap_start(*row_swap(base_bias, 5))
    swap_wait(*fold_swap(*near_first))
    swap_wait(*fold_swap(*near_next))
    swap_wait(*fold_swap(*near_rest))
    swap_wait(*row_swap(code, 1))
    swap_wait(*row_swap(bias.at[0], 2))
    swap_wait(*state_swap(2, False))
    two_steps(0, 2)
    swap_start(*state_swap(3, False))
    swap_start(*fold_swap(*far_first))
    swap_wait(*state_swap(3, False))
    two_steps(0, 3)
    swap_start(*state_swap(4, True))
    send_forces(0, 4)
    swap_start(*fold_swap(*far_rest))

    swap_wait(*pack_swap(4))
    swap_wait(*row_swap(base_bias, 5))
    for b in (1, 2):
        near_pack = pack_near.at[b - 1]
        tables(
            b,
            lambda t: near_pack[ROWS + NVAR + t : ROWS + NVAR + t + 1].astype(jnp.int32),
            lambda t: near_pack[NVAR + t : NVAR + t + 1],
            near_pack[2 * ROWS + NVAR : 2 * ROWS + NVAR + 1].astype(jnp.int32),
        )
    swap_wait(*fold_swap(*far_first))
    swap_wait(*fold_swap(*far_rest))
    swap_wait(*state_swap(4, True))
    for f in (0, ROWS):
        outer = sweep(state.at[4], f, [jnp.zeros((ROWS, LANE), jnp.float32)] * NVAR)
        for v in range(NVAR):
            partial[v, f : f + ROWS] = outer[v]
    solve(0)
    landing = struct_all.at[1, pl.ds(pl.multiple_of(own_row, piece), piece)]
    all_start(lambda p: result.at[0], landing, gather_send, gather_recv)
    struct_all[1, pl.ds(pl.multiple_of(own_row, piece), piece)] = result[0]
    all_wait(struct_all.at[1, 0 : shell_total - piece], gather_send, gather_recv)

    couple(1, (0, 1, 2))
    for f in (0, ROWS):
        into_work(f, [partial[v, f : f + ROWS] + bias[1, v, f : f + ROWS] for v in range(NVAR)])
    last_steps(1, 5)
    swap_start(*state_swap(5, True))
    shell_terms(1)
    swap_wait(*state_swap(5, True))
    three_steps(1, 5)
    last = send_forces(1, 6)
    fluid_ref[...] = last
    solve(1)

    def final_copy(r, landing):
        return pltpu.make_async_remote_copy(
            src_ref=result.at[1],
            dst_ref=final_land.at[landing],
            send_sem=final_send.at[r],
            recv_sem=final_recv.at[landing],
            device_id=(peers_f[r], me_s),
            device_id_type=MESH,
        )

    for r in range(1, fluid_n):
        final_copy(r, me_f).start()
    final_land[me_f] = result[1]
    for r in range(1, fluid_n):
        final_copy(r, peers_f[r]).wait()
    for f in range(fluid_n):
        struct_ref[f * piece : (f + 1) * piece] = final_land[f]


def finish(fluid_in, struct_in, fluid_ref, struct_ref):
    fluid_ref[...] = fluid_in[...]
    per = FOLD // BLK
    groups = struct_in.shape[0] // per
    wide = jnp.concatenate(
        [struct_in[pl.ds(q, groups, stride=per)][:, 0:BLK] for q in range(per)], axis=1
    )
    for q in range(FOLD // LANE):
        struct_ref[pl.ds(q, groups, stride=FOLD // LANE)] = wide[:, q * LANE : (q + 1) * LANE]


def body(
    fluid_n,
    struct_n,
    fluid_adjoint,
    fluid_rhs,
    diag_inverse,
    face_blocks,
    face_index,
    surface_cell,
    surface_count,
    transfer_node,
    transfer_weight,
    load_sens,
    disp_sens,
    struct_adjoint,
    struct_rhs,
    shell_blocks,
    shell_inverse,
    shell_columns,
):
    cells = fluid_adjoint.shape[1]
    slots = surface_cell.shape[0]
    block_rows = struct_adjoint.shape[0] // BLK
    shell_total = block_rows * struct_n
    piece = block_rows // fluid_n
    total = fluid_n * struct_n
    tiles = cells // LANE
    vmem = pl.BlockSpec(memory_space=pltpu.VMEM)
    far = pl.BlockSpec(memory_space=pl.ANY)
    f32, bf16 = jnp.float32, jnp.bfloat16
    dma = pltpu.SemaphoreType.DMA

    fluid_out, struct_out = pl.pallas_call(
        functools.partial(kernel, fluid_n, struct_n, piece),
        out_shape=(
            jax.ShapeDtypeStruct((NVAR, cells), f32),
            jax.ShapeDtypeStruct((block_rows, LANE), f32),
        ),
        in_specs=[far] * 6 + [vmem] + [far] * 9,
        out_specs=(vmem, vmem),
        scratch_shapes=[
            pltpu.VMEM((7, NVAR, 3 * ROWS, LANE), f32),
            pltpu.VMEM((NVAR, 3 * ROWS, LANE), f32),
            pltpu.VMEM((FACES * NVAR * NVAR, 2 * ROWS, LANE), f32),
            pltpu.VMEM((FACES, 2 * ROWS, LANE), jnp.int32),
            pltpu.VMEM((FACES // 2 * NVAR * NVAR, ROWS, LANE), f32),
            pltpu.VMEM((FACES // 2, ROWS, LANE), jnp.int32),
            pltpu.VMEM((NVAR, 2 * ROWS, LANE), f32),
            pltpu.VMEM((ITERS, NVAR, 2 * ROWS, LANE), f32),
            pltpu.VMEM((NVAR, 2 * ROWS, LANE), f32),
            pltpu.VMEM((tiles * ROWS, LANE), f32),
            pltpu.VMEM((tiles * ROWS, LANE), jnp.int32),
            pltpu.VMEM((NVAR * NVAR * tiles * ROWS, LANE), f32),
            pltpu.VMEM((NVAR * ROWS, cells), f32),
            pltpu.VMEM((3 * ROWS, slots), f32),
            pltpu.VMEM((2, 3 * ROWS, slots), f32),
            pltpu.VMEM((3, cells, slots), bf16),
            pltpu.VMEM((3, shell_total, TMAP * slots), bf16),
            pltpu.VMEM((3, NPB, TMAP * slots), f32),
            pltpu.VMEM((NB, ROWS, BLK * BLK), f32),
            pltpu.VMEM((ROWS, BLK * BLK), f32),
            pltpu.VMEM((LANE, BLK * BLK), bf16),
            pltpu.VMEM((block_rows, LANE), f32),
            pltpu.VMEM((block_rows, LANE), f32),
            pltpu.VMEM((ITERS, shell_total, LANE), f32),
            pltpu.VMEM((NB * ROWS, LANE), f32),
            pltpu.VMEM((ROWS, LANE), f32),
            pltpu.VMEM((ITERS, shell_total, LANE), f32),
            pltpu.VMEM((ITERS, total, piece, LANE), f32),
            pltpu.VMEM((ITERS, piece, LANE), f32),
            pltpu.VMEM((fluid_n, piece, LANE), f32),
            dma((6, 4)),
            dma((6, 4)),
            dma((9, 2)),
            dma((9, 2)),
            dma((struct_n,)),
            dma((struct_n,)),
            dma((ITERS,)),
            dma((ITERS,)),
            dma,
            dma,
            dma((fluid_n,)),
            dma((fluid_n,)),
            dma((NB + 1,)),
            dma((13,)),
            pltpu.VMEM((NVAR, cells), f32),
            pltpu.VMEM((NVAR, cells), f32),
            pltpu.VMEM((NVAR, NVAR, cells), f32),
            pltpu.VMEM((NVAR, NVAR, FACES, cells), f32),
            pltpu.VMEM((FACES, cells), jnp.int32),
            pltpu.VMEM((1, slots), jnp.int32),
            pltpu.VMEM((TMAP, slots), jnp.int32),
            pltpu.VMEM((TMAP, slots), f32),
            pltpu.VMEM((NVAR, 3, slots), f32),
            pltpu.VMEM((NVAR, 3, slots), f32),
            pltpu.VMEM((block_rows * BLK // LANE, LANE), f32),
            pltpu.VMEM((block_rows * BLK // LANE, LANE), f32),
            pltpu.SMEM((NB, block_rows), jnp.int32),
        ],
        compiler_params=pltpu.CompilerParams(collective_id=0, has_side_effects=True),
    )(
        fluid_adjoint,
        fluid_rhs,
        diag_inverse,
        jnp.transpose(face_blocks, (1, 2, 0, 3)),
        face_index,
        surface_cell.reshape(1, slots),
        surface_count.reshape(1, 1),
        transfer_node,
        transfer_weight,
        jnp.transpose(load_sens, (1, 0, 2)),
        disp_sens,
        struct_adjoint.reshape(-1, LANE),
        struct_rhs.reshape(-1, LANE),
        shell_blocks,
        shell_inverse,
        shell_columns,
    )
    fluid_out, struct_out = pl.pallas_call(
        finish,
        out_shape=(
            jax.ShapeDtypeStruct((NVAR, cells), f32),
            jax.ShapeDtypeStruct((block_rows * BLK // LANE, LANE), f32),
        ),
        in_specs=[vmem, vmem],
        out_specs=(vmem, vmem),
    )(fluid_out, struct_out)
    return fluid_out, struct_out.reshape(-1)


def solution(mesh):
    placed = (
        P(None, ("fluid", "struct")),
        P(None, ("fluid", "struct")),
        P(None, None, ("fluid", "struct")),
        P(None, None, None, ("fluid", "struct")),
        P(None, ("fluid", "struct")),
        P(("fluid", "struct")),
        P(("fluid", "struct")),
        P(None, ("fluid", "struct")),
        P(None, ("fluid", "struct")),
        P(None, None, ("fluid", "struct")),
        P(None, None, ("fluid", "struct")),
        P("struct"),
        P("struct"),
        P(None, "struct", None),
        P("struct", None),
        P(None, "struct"),
    )
    return jax.shard_map(
        functools.partial(body, mesh.shape["fluid"], mesh.shape["struct"]),
        mesh=mesh,
        in_specs=placed,
        out_specs=(P(None, ("fluid", "struct")), P("struct")),
        check_vma=False,
    )
```

time: 66.4 us -> 56.4 us (0.85)
  Pallas kernels: 64.8 us -> 54.8 us
    pallas_call x1, Pallas kernels: 63.4 us -> 53.4 us  [body(): pl.pallas_call(functools.partial(kernel, fluid_n, struct_n, piece), out_s...]
where the time goes in v2:
time: 56.4 us; the launch traced here: 56.1 us
  Pallas kernels  54.8 us (97%)
  between operations  1.29 us (2%)
    pallas_call x1, Pallas kernels, body(): pl.pallas_call(functools.partial(kernel, fluid_n, struct_n, piece), out_s...  53.4 us
    pallas_call x1, Pallas kernels, body(): pl.pallas_call(finish, out_shape=(jax.ShapeDtypeStruct((NVAR, cells), f32...  1.41 us

profile of v2, /device:TPU:0, one launch (start us, length us, event | category | flops | bytes accessed | tf_op | source)
XLA Modules:
  0.0 56.1 jit_solution(17791377123777125577)
XLA Ops:
  1.3 53.4 %shard_map.167 = (f32[5,512]{1,0:T(8,128)}, f32[32,128]{1,0:T(8,128)}) custom-call(f32[5,512]{1,0:T(8,128)} %adj_far.1, f32[5,512]{1,0:T(8,128)} %rhs_far.1, f32[5,5,512]{2,1,0:T(8,128)} %diag_far.1, f32[5,5,6,512]{3,2,1,0:T(8,128)} %bitcast.8, s32[6,512]{1,0:T(8,128)} %index_far.1, s32[1,256]{1,0:T(1,128)} %bitcast.12, s32[1,1]{1,0:T(1,128)} %bitcast.7.count_ref, ...), custom_call_target="tpu_custom_call" | custom-call | tf_op jit(solution)/shard_map/pallas_call | solution.py:772
  54.7 1.4 %shard_map.168 = (f32[5,512]{1,0:T(8,128)}, f32[24,128]{1,0:T(8,128)}) custom-call(f32[5,512]{1,0:T(8,128)} %get-tuple-element.6.fluid_in, f32[32,128]{1,0:T(8,128)} %get-tuple-element.7.struct_in), custom_call_target="tpu_custom_call" | custom-call | tf_op jit(solution)/shard_map/pallas_call | solution.py:858

commit v3 on v2

--- a/solution.py
+++ b/solution.py
@@ -116,7 +116,9 @@
     right_struct,
     struct_all,
     rows_x,
-    terms,
+    known,
+    flat,
+    mats,
     forces_out,
     forces_land,
     result,
@@ -343,6 +345,7 @@
     by_block(sadj_ref, start_struct)
     by_block(srhs_ref, right_struct)
     forces_out[...] = jnp.zeros_like(forces_out)
+    result[...] = jnp.zeros_like(result)
 
     pl.semaphore_wait(barrier, total - 1)
 
@@ -588,7 +591,7 @@
                 product = wide[m * ROWS : (m + 1) * ROWS] * blocks[m, :, c : c + CHUNK]
                 for g in range(0, CHUNK, FOLD):
                     acc = acc + product[:, g : g + FOLD]
-        terms[...] = dot_left(acc, fold, NN)
+        known[...] = right_struct[pl.ds(pl.multiple_of(base, ROWS), ROWS)] - dot_left(acc, fold, NN)
 
     def send_forces(i, e):
         for v in range(NVAR):
@@ -619,25 +622,37 @@
 
     def solve(i):
         all_wait(forces_land.at[i, 0 : total - 1], force_send.at[i], force_recv.at[i])
-        mine = forces_land[i, 0]
-        for q in range(1, total):
-            mine = mine + forces_land[i, q]
-        mine = jnp.concatenate([mine] * (ROWS // piece), axis=0)
+        pieces = [forces_land[i, q] for q in range(total)]
+        while len(pieces) > 1:
+            pieces = [sum(pieces[q : q + 2][1:], pieces[q]) for q in range(0, len(pieces), 2)]
+        mine = jnp.concatenate(pieces * (ROWS // piece), axis=0)
         spread = dot_left(mine[:, 0 : 2 * width], perm_twice, NN)
-        load = right_struct[pl.ds(pl.multiple_of(base, ROWS), ROWS)] + spread - terms[...]
-        tiled = dot_left(load, fold, NT)
-        solved = jnp.zeros((2 * ROWS, LANE), jnp.float32)
-        for c in range(0, BLK * BLK, CHUNK):
-            product = inverse[:, c : c + CHUNK] * jnp.concatenate([tiled] * (CHUNK // FOLD), axis=1)
-            parts = jnp.concatenate(
-                [p.astype(jnp.float32) for p in split(product)], axis=0
-            ).astype(jnp.bfloat16)
-            solved = solved + dot(parts, expand[:, c : c + CHUNK], NT)
-        solved = solved[0:ROWS] + solved[ROWS:]
+        load = known[pl.ds(pl.multiple_of(my_row - base, piece), piece)] + spread[0:piece]
+        high, low = [p.astype(jnp.float32) for p in split(load)]
+        parts = jnp.concatenate(
+            [
+                jnp.concatenate([high, high], axis=1),
+                jnp.concatenate([low, jnp.zeros_like(low)], axis=1),
+            ],
+            axis=0,
+        ).astype(jnp.bfloat16)
+        for r in range(piece):
+            out = dot(parts, mats[r], NT)
+            result[i, r : r + 1, 0:BLK] = out[r : r + 1] + out[piece + r : piece + r + 1]
+
+    def matrices():
+        for p in range(BLK):
+            flat[p * ROWS : (p + 1) * ROWS] = jnp.concatenate(
+                [inverse[:, p * BLK : (p + 1) * BLK], jnp.zeros((ROWS, LANE - BLK), jnp.float32)],
+                axis=1,
+            )
         for g in range(ROWS // piece):
             @pl.when(my_row - base == g * piece)
             def _():
-                result[i] = solved[g * piece : (g + 1) * piece]
+                for r in range(piece):
+                    high, low = split(flat[pl.ds(g * piece + r, BLK, stride=ROWS)])
+                    mats[r, :, 0:LANE] = high
+                    mats[r, :, LANE : 2 * LANE] = low
 
     swap_wait(*state_swap(0, False))
     early = own_sweep(state.at[0])
@@ -651,6 +666,7 @@
     swap_start(*row_swap(bias.at[0], 2))
     swap_start(*fold_swap(*near_next))
     shell_terms(0)
+    matrices()
     swap_wait(*state_swap(1, False))
     own_step(0, 2, state.at[1])
     swap_start(*state_swap(2, False))
@@ -682,6 +698,10 @@
             lambda t: near_pack[NVAR + t : NVAR + t + 1],
             near_pack[2 * ROWS + NVAR : 2 * ROWS + NVAR + 1].astype(jnp.int32),
         )
+    solve(0)
+    landing = struct_all.at[1, pl.ds(pl.multiple_of(own_row, piece), piece)]
+    all_start(lambda p: result.at[0], landing, gather_send, gather_recv)
+    struct_all[1, pl.ds(pl.multiple_of(own_row, piece), piece)] = result[0]
     swap_wait(*fold_swap(*far_first))
     swap_wait(*fold_swap(*far_rest))
     swap_wait(*state_swap(4, True))
@@ -689,10 +709,6 @@
         outer = sweep(state.at[4], f, [jnp.zeros((ROWS, LANE), jnp.float32)] * NVAR)
         for v in range(NVAR):
             partial[v, f : f + ROWS] = outer[v]
-    solve(0)
-    landing = struct_all.at[1, pl.ds(pl.multiple_of(own_row, piece), piece)]
-    all_start(lambda p: result.at[0], landing, gather_send, gather_recv)
-    struct_all[1, pl.ds(pl.multiple_of(own_row, piece), piece)] = result[0]
     all_wait(struct_all.at[1, 0 : shell_total - piece], gather_send, gather_recv)
 
     couple(1, (0, 1, 2))
@@ -804,6 +820,8 @@
             pltpu.VMEM((ITERS, shell_total, LANE), f32),
             pltpu.VMEM((NB * ROWS, LANE), f32),
             pltpu.VMEM((ROWS, LANE), f32),
+            pltpu.VMEM((BLK * ROWS, LANE), f32),
+            pltpu.VMEM((piece, BLK, 2 * LANE), bf16),
             pltpu.VMEM((ITERS, shell_total, LANE), f32),
             pltpu.VMEM((ITERS, total, piece, LANE), f32),
             pltpu.VMEM((ITERS, piece, LANE), f32),

time: 56.4 us -> 52.1 us (0.924)
  Pallas kernels: 54.8 us -> 50.5 us
    pallas_call x1, Pallas kernels: 53.4 us -> 49.1 us  [body(): pl.pallas_call(functools.partial(kernel, fluid_n, struct_n, piece), out_s...]
where the time goes in v3:
time: 52.1 us; the launch traced here: 51.8 us
  Pallas kernels  50.5 us (97%)
  between operations  1.29 us (2%)
    pallas_call x1, Pallas kernels, body(): pl.pallas_call(functools.partial(kernel, fluid_n, struct_n, piece), out_s...  49.1 us
    pallas_call x1, Pallas kernels, body(): pl.pallas_call(finish, out_shape=(jax.ShapeDtypeStruct((NVAR, cells), f32...  1.41 us

profile of v3, /device:TPU:0, one launch (start us, length us, event | category | flops | bytes accessed | tf_op | source)
XLA Modules:
  0.0 51.8 jit_solution(14839306742733677380)
XLA Ops:
  1.3 49.1 %shard_map.167 = (f32[5,512]{1,0:T(8,128)}, f32[32,128]{1,0:T(8,128)}) custom-call(f32[5,512]{1,0:T(8,128)} %adj_far.1, f32[5,512]{1,0:T(8,128)} %rhs_far.1, f32[5,5,512]{2,1,0:T(8,128)} %diag_far.1, f32[5,5,6,512]{3,2,1,0:T(8,128)} %bitcast.8, s32[6,512]{1,0:T(8,128)} %index_far.1, s32[1,256]{1,0:T(1,128)} %bitcast.12, s32[1,1]{1,0:T(1,128)} %bitcast.7.count_ref, ...), custom_call_target="tpu_custom_call" | custom-call | tf_op jit(solution)/shard_map/pallas_call | solution.py:788
  50.4 1.4 %shard_map.168 = (f32[5,512]{1,0:T(8,128)}, f32[24,128]{1,0:T(8,128)}) custom-call(f32[5,512]{1,0:T(8,128)} %get-tuple-element.6.fluid_in, f32[32,128]{1,0:T(8,128)} %get-tuple-element.7.struct_in), custom_call_target="tpu_custom_call" | custom-call | tf_op jit(solution)/shard_map/pallas_call | solution.py:876

commit v4 on v3

--- a/solution.py
+++ b/solution.py
@@ -107,6 +107,7 @@
     pack,
     pack_near,
     cell_table,
+    slot_map,
     block_table,
     node_mask,
     blocks,
@@ -340,7 +341,7 @@
 
     for copy in inputs[0:3]:
         copy.wait()
-    for v, value in enumerate(to_rows(adj_ref[...], mix, NVAR)):
+    for v, value in enumerate(to_rows(adj_ref[...], mix.at[0], NVAR)):
         state[0, v, own_x : own_x + tiles] = value
     by_block(sadj_ref, start_struct)
     by_block(srhs_ref, right_struct)
@@ -396,7 +397,9 @@
     swap_start(*row_swap(code, 1))
 
     def tables(b, node_of, weight_of, cell_of):
-        cell_table[b] = jnp.where(iota((cells, slots), 0) == cell_of, 1.0, 0.0).astype(jnp.bfloat16)
+        cell_table[...] = jnp.where(iota((cells, slots), 0) == cell_of, 1.0, 0.0).astype(jnp.bfloat16)
+        ids = (iota((ROWS, slots), 1) + 1).astype(jnp.float32)
+        slot_map[b] = dot_left(ids, cell_table[...], NT).astype(jnp.int32)
         for t in range(TMAP):
             node = node_of(t)
             block_of = lax.shift_right_logical(node, NPB.bit_length() - 1)
@@ -414,7 +417,7 @@
     for u in range(NVAR):
         for v in range(NVAR):
             diag_mix[u * ROWS + v : u * ROWS + v + 1] = diag_ref[v, u : u + 1]
-    at_slots = dot_left(diag_mix[...], cell_table[0], NN)
+    at_slots = dot_left(diag_mix[...], cell_table[...], NN)
     for j in range(3):
         out = at_slots[0:NVAR] * load_ref[0, j : j + 1]
         for u in range(1, NVAR):
@@ -431,11 +434,6 @@
         for a in range(tiles):
             base_bias[v, own + a : own + a + 1] = mixed[:, span(a)]
 
-    for c in range(0, BLK * BLK, CHUNK):
-        offset = iota((LANE, CHUNK), 1) + c - BLK * iota((LANE, CHUNK), 0)
-        expand[:, c : c + CHUNK] = jnp.where((offset >= 0) & (offset < BLK), 1.0, 0.0).astype(
-            jnp.bfloat16
-        )
     width = 3 * NPB
     out_row = iota((width, LANE), 0)
     perm = jnp.where(
@@ -518,11 +516,20 @@
         into_work(ROWS, outer[1])
         last_steps(i, e + 1)
 
+    def gather_rows(sources, place):
+        lane = place & (LANE - 1)
+        tile = lax.shift_right_logical(place, LANE.bit_length() - 1)
+        out = None
+        for c, source in enumerate(sources):
+            found = jnp.take_along_axis(source, lane, axis=1, mode="promise_in_bounds")
+            out = found if out is None else jnp.where(tile == c, found, out)
+        return out
+
     def couple(i, which):
-        by_node = dot_right(perm, struct_all[i], NT)
-        parts = jnp.concatenate([p.astype(jnp.float32) for p in split(by_node)], axis=0).astype(
-            jnp.bfloat16
-        )
+        by_node = dot(perm, jnp.concatenate(split(struct_all[i]), axis=0), NT)
+        parts = jnp.concatenate(
+            [by_node[:, 0:shell_total], by_node[:, shell_total : 2 * shell_total]], axis=0
+        ).astype(jnp.bfloat16)
         for b in which:
             picked = dot(parts, block_table[b], NN)
             picked = picked[0:width] + picked[width : 2 * width]
@@ -538,9 +545,13 @@
             coupled = rates[0:ROWS] * displaced[0:1]
             for j in range(1, 3):
                 coupled = coupled + rates[j * ROWS : (j + 1) * ROWS] * displaced[j : j + 1]
-            spread = dot_left(coupled, cell_table[b], NT)
+            spread = []
+            for a in range(tiles):
+                place = slot_map[b, :, span(a)]
+                found = gather_rows([coupled[:, span(c)] for c in range(slots // LANE)], place - 1)
+                spread.append(jnp.where(place > 0, found, 0.0))
             first = (own, 0, own + tiles)[b]
-            for v, value in enumerate(to_rows(spread[0:NVAR], mix, NVAR)):
+            for v, value in enumerate(to_rows(jnp.concatenate(spread, axis=1)[0:NVAR], mix.at[b], NVAR)):
                 bias[i, v, first : first + tiles] = base_bias[v, first : first + tiles] + value
 
     def all_start(source, landing, send, recv):
@@ -595,11 +606,13 @@
 
     def send_forces(i, e):
         for v in range(NVAR):
-            mix[v * tiles : (v + 1) * tiles] = state[e, v, own_x : own_x + tiles]
-        last = jnp.concatenate(
-            [mix[pl.ds(a, NVAR, stride=tiles)] for a in range(tiles)], axis=1
-        )
-        at_surface = dot_left(pad_rows(last), cell_table[0], NN)
+            mix[0, v * tiles : (v + 1) * tiles] = state[e, v, own_x : own_x + tiles]
+        parts = [pad_rows(mix[0, pl.ds(a, NVAR, stride=tiles)]) for a in range(tiles)]
+        last = jnp.concatenate([p[0:NVAR] for p in parts], axis=1)
+        place = jnp.broadcast_to(cell_ref[...], (ROWS, slots))
+        at_surface = jnp.concatenate(
+            [gather_rows(parts, place[:, span(c)]) for c in range(slots // LANE)], axis=1
+        )
         sens = jnp.zeros((3, slots), jnp.float32)
         for v in range(NVAR):
             sens = sens + disp_ref[v] * at_surface[v : v + 1]
@@ -665,14 +678,19 @@
     swap_start(*state_swap(1, False))
     swap_start(*row_swap(bias.at[0], 2))
     swap_start(*fold_swap(*near_next))
+    for c in range(0, BLK * BLK, CHUNK):
+        offset = iota((LANE, CHUNK), 1) + c - BLK * iota((LANE, CHUNK), 0)
+        expand[:, c : c + CHUNK] = jnp.where((offset >= 0) & (offset < BLK), 1.0, 0.0).astype(
+            jnp.bfloat16
+        )
     shell_terms(0)
-    matrices()
     swap_wait(*state_swap(1, False))
     own_step(0, 2, state.at[1])
     swap_start(*state_swap(2, False))
     swap_start(*fold_swap(*near_rest))
     swap_start(*pack_swap(4))
     swap_start(*row_swap(base_bias, 5))
+    matrices()
     swap_wait(*fold_swap(*near_first))
     swap_wait(*fold_swap(*near_next))
     swap_wait(*fold_swap(*near_rest))
@@ -803,13 +821,14 @@
             pltpu.VMEM((NVAR, 2 * ROWS, LANE), f32),
             pltpu.VMEM((ITERS, NVAR, 2 * ROWS, LANE), f32),
             pltpu.VMEM((NVAR, 2 * ROWS, LANE), f32),
-            pltpu.VMEM((tiles * ROWS, LANE), f32),
+            pltpu.VMEM((3, tiles * ROWS, LANE), f32),
             pltpu.VMEM((tiles * ROWS, LANE), jnp.int32),
             pltpu.VMEM((NVAR * NVAR * tiles * ROWS, LANE), f32),
             pltpu.VMEM((NVAR * ROWS, cells), f32),
             pltpu.VMEM((3 * ROWS, slots), f32),
             pltpu.VMEM((2, 3 * ROWS, slots), f32),
-            pltpu.VMEM((3, cells, slots), bf16),
+            pltpu.VMEM((cells, slots), bf16),
+            pltpu.VMEM((3, ROWS, cells), jnp.int32),
             pltpu.VMEM((3, shell_total, TMAP * slots), bf16),
             pltpu.VMEM((3, NPB, TMAP * slots), f32),
             pltpu.VMEM((NB, ROWS, BLK * BLK), f32),

time: 52.1 us -> 51.5 us (0.988)
  Pallas kernels: 50.5 us -> 49.9 us
    pallas_call x1, Pallas kernels: 49.1 us -> 48.5 us  [body(): pl.pallas_call(functools.partial(kernel, fluid_n, struct_n, piece), out_s...]
where the time goes in v4:
time: 51.5 us; the launch traced here: 51.2 us
  Pallas kernels  49.9 us (97%)
  between operations  1.29 us (3%)
    pallas_call x1, Pallas kernels, body(): pl.pallas_call(functools.partial(kernel, fluid_n, struct_n, piece), out_s...  48.5 us
    pallas_call x1, Pallas kernels, body(): pl.pallas_call(finish, out_shape=(jax.ShapeDtypeStruct((NVAR, cells), f32...  1.41 us

profile of v4, /device:TPU:0, one launch (start us, length us, event | category | flops | bytes accessed | tf_op | source)
XLA Modules:
  0.0 51.2 jit_solution(11044854963197781774)
XLA Ops:
  1.3 48.5 %shard_map.167 = (f32[5,512]{1,0:T(8,128)}, f32[32,128]{1,0:T(8,128)}) custom-call(f32[5,512]{1,0:T(8,128)} %adj_far.1, f32[5,512]{1,0:T(8,128)} %rhs_far.1, f32[5,5,512]{2,1,0:T(8,128)} %diag_far.1, f32[5,5,6,512]{3,2,1,0:T(8,128)} %bitcast.8, s32[6,512]{1,0:T(8,128)} %index_far.1, s32[1,256]{1,0:T(1,128)} %bitcast.12, s32[1,1]{1,0:T(1,128)} %bitcast.7.count_ref, ...), custom_call_target="tpu_custom_call" | custom-call | tf_op jit(solution)/shard_map/pallas_call | solution.py:806
  49.8 1.4 %shard_map.168 = (f32[5,512]{1,0:T(8,128)}, f32[24,128]{1,0:T(8,128)}) custom-call(f32[5,512]{1,0:T(8,128)} %get-tuple-element.6.fluid_in, f32[32,128]{1,0:T(8,128)} %get-tuple-element.7.struct_in), custom_call_target="tpu_custom_call" | custom-call | tf_op jit(solution)/shard_map/pallas_call | solution.py:895

commit v5 on v4

--- a/solution.py
+++ b/solution.py
@@ -136,6 +136,7 @@
     gather_recv,
     final_send,
     final_recv,
+    round_sem,
     local_sem,
     input_sem,
     adj_ref,
@@ -174,12 +175,34 @@
     peers_f = [(me_f + r) % fluid_n for r in range(fluid_n)]
     peers_s = [(me_s + r) % struct_n for r in range(struct_n)]
     barrier = pltpu.get_barrier_semaphore()
-    for rf in reversed(range(fluid_n)):
-        for rs in reversed(range(struct_n)):
-            if rf + rs:
-                pl.semaphore_signal(
-                    barrier, inc=1, device_id=(peers_f[rf], peers_s[rs]), device_id_type=MESH
-                )
+    bits = [1 << d for d in range(fluid_n.bit_length() - 1)]
+    partners = [(me_f + j - 2 * j * ((me_f // j) % 2), me_s) for j in bits]
+
+    def greet(semaphore, device):
+        pl.semaphore_signal(semaphore, inc=1, device_id=device, device_id_type=MESH)
+
+    last_s = struct_n - 1
+
+    @pl.when(me_s == last_s)
+    def _():
+        greet(barrier, (peers_f[1], 0))
+
+    @pl.when(me_s == 0)
+    def _():
+        greet(barrier, (peers_f[fluid_n - 1], last_s))
+
+    for r in range(1, struct_n):
+        greet(barrier, (me_f, peers_s[r]))
+    for partner in partners:
+        greet(barrier, partner)
+    ends = jnp.where(me_s == 0, 1, 0) + jnp.where(me_s == last_s, 1, 0)
+
+    def round_start(n):
+        for partner in partners:
+            greet(round_sem.at[n], partner)
+
+    def round_wait(n):
+        pl.semaphore_wait(round_sem.at[n], len(partners))
 
     inputs = []
     for n, (source, landing) in enumerate(
@@ -307,48 +330,14 @@
     def clear(ref, first, count):
         ref[:, first : first + count] = jnp.zeros((ref.shape[0], count, LANE), ref.dtype)
 
-    spare = state.shape[2]
-    for e in range(state.shape[0]):
-        clear(state.at[e], own_x + 2 * tiles + half, spare - own_x - 2 * tiles - half)
-
-        @pl.when(me == 0)
-        def _():
-            clear(state.at[e], 0, own_x)
-
-        @pl.when(me == 1)
-        def _():
-            clear(state.at[e], 0, half)
-
-        @pl.when(me == total - 2)
-        def _():
-            clear(state.at[e], own_x + 2 * tiles, half)
-
-        @pl.when(me == total - 1)
-        def _():
-            clear(state.at[e], own_x + tiles, tiles + half)
-
-    @pl.when(me == 0)
-    def _():
-        for ref in (folded, code, base_bias, bias.at[0]):
-            clear(ref, 0, tiles)
-        pack_near[0] = jnp.zeros_like(pack)
-
-    @pl.when(me == total - 1)
-    def _():
-        for ref in (folded, code, base_bias, bias.at[0]):
-            clear(ref, own + tiles, tiles)
-        pack_near[1] = jnp.zeros_like(pack)
-
     for copy in inputs[0:3]:
         copy.wait()
     for v, value in enumerate(to_rows(adj_ref[...], mix.at[0], NVAR)):
         state[0, v, own_x : own_x + tiles] = value
     by_block(sadj_ref, start_struct)
-    by_block(srhs_ref, right_struct)
-    forces_out[...] = jnp.zeros_like(forces_out)
-    result[...] = jnp.zeros_like(result)
-
-    pl.semaphore_wait(barrier, total - 1)
+
+    pl.semaphore_wait(barrier, struct_n - 1 + len(partners) + ends)
+    round_start(0)
 
     def start_copy(r, landing):
         return pltpu.make_async_remote_copy(
@@ -363,6 +352,41 @@
     for r in range(1, struct_n):
         start_copy(r, me_s).start()
     swap_start(*state_swap(0, False))
+    spare = state.shape[2]
+    for e in range(state.shape[0]):
+        clear(state.at[e], own_x + 2 * tiles + half, spare - own_x - 2 * tiles - half)
+
+        @pl.when(me == 0)
+        def _():
+            clear(state.at[e], 0, own_x)
+
+        @pl.when(me == 1)
+        def _():
+            clear(state.at[e], 0, half)
+
+        @pl.when(me == total - 2)
+        def _():
+            clear(state.at[e], own_x + 2 * tiles, half)
+
+        @pl.when(me == total - 1)
+        def _():
+            clear(state.at[e], own_x + tiles, tiles + half)
+
+    @pl.when(me == 0)
+    def _():
+        for ref in (folded, code, base_bias, bias.at[0]):
+            clear(ref, 0, tiles)
+        pack_near[0] = jnp.zeros_like(pack)
+
+    @pl.when(me == total - 1)
+    def _():
+        for ref in (folded, code, base_bias, bias.at[0]):
+            clear(ref, own + tiles, tiles)
+        pack_near[1] = jnp.zeros_like(pack)
+
+    by_block(srhs_ref, right_struct)
+    forces_out[...] = jnp.zeros_like(forces_out)
+    result[...] = jnp.zeros_like(result)
 
     for copy in inputs[3:]:
         copy.wait()
@@ -685,6 +709,8 @@
         )
     shell_terms(0)
     swap_wait(*state_swap(1, False))
+    round_wait(0)
+    round_start(1)
     own_step(0, 2, state.at[1])
     swap_start(*state_swap(2, False))
     swap_start(*fold_swap(*near_rest))
@@ -697,10 +723,16 @@
     swap_wait(*row_swap(code, 1))
     swap_wait(*row_swap(bias.at[0], 2))
     swap_wait(*state_swap(2, False))
+    round_wait(1)
+    round_start(2)
     two_steps(0, 2)
     swap_start(*state_swap(3, False))
     swap_start(*fold_swap(*far_first))
     swap_wait(*state_swap(3, False))
+    round_wait(2)
+    for n in range(3, len(bits)):
+        round_start(n)
+        round_wait(n)
     two_steps(0, 3)
     swap_start(*state_swap(4, True))
     send_forces(0, 4)
@@ -857,6 +889,7 @@
             dma,
             dma((fluid_n,)),
             dma((fluid_n,)),
+            pltpu.SemaphoreType.REGULAR((max(3, fluid_n.bit_length() - 1),)),
             dma((NB + 1,)),
             dma((13,)),
             pltpu.VMEM((NVAR, cells), f32),

time: 51.5 us -> 49.9 us (0.969)
  Pallas kernels: 49.9 us -> 48.3 us
    pallas_call x1, Pallas kernels: 48.5 us -> 46.9 us  [body(): pl.pallas_call(functools.partial(kernel, fluid_n, struct_n, piece), out_s...]
where the time goes in v5:
time: 49.9 us; the launch traced here: 49.6 us
  Pallas kernels  48.3 us (97%)
  between operations  1.29 us (3%)
    pallas_call x1, Pallas kernels, body(): pl.pallas_call(functools.partial(kernel, fluid_n, struct_n, piece), out_s...  46.9 us
    pallas_call x1, Pallas kernels, body(): pl.pallas_call(finish, out_shape=(jax.ShapeDtypeStruct((NVAR, cells), f32...  1.41 us

profile of v5, /device:TPU:0, one launch (start us, length us, event | category | flops | bytes accessed | tf_op | source)
XLA Modules:
  0.0 49.6 jit_solution(16981817043119342334)
XLA Ops:
  1.3 46.9 %shard_map.167 = (f32[5,512]{1,0:T(8,128)}, f32[32,128]{1,0:T(8,128)}) custom-call(f32[5,512]{1,0:T(8,128)} %adj_far.1, f32[5,512]{1,0:T(8,128)} %rhs_far.1, f32[5,5,512]{2,1,0:T(8,128)} %diag_far.1, f32[5,5,6,512]{3,2,1,0:T(8,128)} %bitcast.8, s32[6,512]{1,0:T(8,128)} %index_far.1, s32[1,256]{1,0:T(1,128)} %bitcast.12, s32[1,1]{1,0:T(1,128)} %bitcast.7.count_ref, ...), custom_call_target="tpu_custom_call" | custom-call | tf_op jit(solution)/shard_map/pallas_call | solution.py:838
  48.2 1.4 %shard_map.168 = (f32[5,512]{1,0:T(8,128)}, f32[24,128]{1,0:T(8,128)}) custom-call(f32[5,512]{1,0:T(8,128)} %get-tuple-element.6.fluid_in, f32[32,128]{1,0:T(8,128)} %get-tuple-element.7.struct_in), custom_call_target="tpu_custom_call" | custom-call | tf_op jit(solution)/shard_map/pallas_call | solution.py:928

commit v6 on v5

--- a/solution.py
+++ b/solution.py
@@ -120,6 +120,8 @@
     known,
     flat,
     mats,
+    plain,
+    ready,
     forces_out,
     forces_land,
     result,
@@ -352,42 +354,6 @@
     for r in range(1, struct_n):
         start_copy(r, me_s).start()
     swap_start(*state_swap(0, False))
-    spare = state.shape[2]
-    for e in range(state.shape[0]):
-        clear(state.at[e], own_x + 2 * tiles + half, spare - own_x - 2 * tiles - half)
-
-        @pl.when(me == 0)
-        def _():
-            clear(state.at[e], 0, own_x)
-
-        @pl.when(me == 1)
-        def _():
-            clear(state.at[e], 0, half)
-
-        @pl.when(me == total - 2)
-        def _():
-            clear(state.at[e], own_x + 2 * tiles, half)
-
-        @pl.when(me == total - 1)
-        def _():
-            clear(state.at[e], own_x + tiles, tiles + half)
-
-    @pl.when(me == 0)
-    def _():
-        for ref in (folded, code, base_bias, bias.at[0]):
-            clear(ref, 0, tiles)
-        pack_near[0] = jnp.zeros_like(pack)
-
-    @pl.when(me == total - 1)
-    def _():
-        for ref in (folded, code, base_bias, bias.at[0]):
-            clear(ref, own + tiles, tiles)
-        pack_near[1] = jnp.zeros_like(pack)
-
-    by_block(srhs_ref, right_struct)
-    forces_out[...] = jnp.zeros_like(forces_out)
-    result[...] = jnp.zeros_like(result)
-
     for copy in inputs[3:]:
         copy.wait()
 
@@ -434,6 +400,42 @@
             node_mask[b, :, t * slots : (t + 1) * slots] = jnp.where(
                 iota((NPB, slots), 0) == inside, weight_of(t), 0.0
             )
+
+    spare = state.shape[2]
+    for e in range(state.shape[0]):
+        clear(state.at[e], own_x + 2 * tiles + half, spare - own_x - 2 * tiles - half)
+
+        @pl.when(me == 0)
+        def _():
+            clear(state.at[e], 0, own_x)
+
+        @pl.when(me == 1)
+        def _():
+            clear(state.at[e], 0, half)
+
+        @pl.when(me == total - 2)
+        def _():
+            clear(state.at[e], own_x + 2 * tiles, half)
+
+        @pl.when(me == total - 1)
+        def _():
+            clear(state.at[e], own_x + tiles, tiles + half)
+
+    @pl.when(me == 0)
+    def _():
+        for ref in (folded, code, base_bias, bias.at[0]):
+            clear(ref, 0, tiles)
+        pack_near[0] = jnp.zeros_like(pack)
+
+    @pl.when(me == total - 1)
+    def _():
+        for ref in (folded, code, base_bias, bias.at[0]):
+            clear(ref, own + tiles, tiles)
+        pack_near[1] = jnp.zeros_like(pack)
+
+    by_block(srhs_ref, right_struct)
+    forces_out[...] = jnp.zeros_like(forces_out)
+    result[...] = jnp.zeros_like(result)
 
     live = (iota((1, slots), 1) < count_ref[...]).astype(jnp.float32)
     tables(0, lambda t: node_ref[t : t + 1], lambda t: weight_ref[t : t + 1], cell_ref[...])
@@ -662,10 +664,11 @@
         pieces = [forces_land[i, q] for q in range(total)]
         while len(pieces) > 1:
             pieces = [sum(pieces[q : q + 2][1:], pieces[q]) for q in range(0, len(pieces), 2)]
-        mine = jnp.concatenate(pieces * (ROWS // piece), axis=0)
-        spread = dot_left(mine[:, 0 : 2 * width], perm_twice, NN)
-        load = known[pl.ds(pl.multiple_of(my_row - base, piece), piece)] + spread[0:piece]
-        high, low = [p.astype(jnp.float32) for p in split(load)]
+        for r, out in enumerate(products(pieces[0], mats)):
+            result[i, r : r + 1, 0:BLK] = ready[r : r + 1, 0:BLK] + out
+
+    def products(value, table):
+        high, low = [p.astype(jnp.float32) for p in split(value)]
         parts = jnp.concatenate(
             [
                 jnp.concatenate([high, high], axis=1),
@@ -673,9 +676,13 @@
             ],
             axis=0,
         ).astype(jnp.bfloat16)
-        for r in range(piece):
-            out = dot(parts, mats[r], NT)
-            result[i, r : r + 1, 0:BLK] = out[r : r + 1] + out[piece + r : piece + r + 1]
+        outs = [dot(parts, table[r], NT) for r in range(piece)]
+        return [out[r : r + 1] + out[piece + r : piece + r + 1] for r, out in enumerate(outs)]
+
+    def solve_known():
+        value = known[pl.ds(pl.multiple_of(my_row - base, piece), piece)]
+        for r, out in enumerate(products(value, plain)):
+            ready[r : r + 1, 0:BLK] = out
 
     def matrices():
         for p in range(BLK):
@@ -688,8 +695,12 @@
             def _():
                 for r in range(piece):
                     high, low = split(flat[pl.ds(g * piece + r, BLK, stride=ROWS)])
-                    mats[r, :, 0:LANE] = high
-                    mats[r, :, LANE : 2 * LANE] = low
+                    for n, part in enumerate((high, low)):
+                        plain[r, :, n * LANE : (n + 1) * LANE] = part
+                        mixed = dot(part, perm_twice, NT)
+                        mats[r, :, n * LANE : (n + 1) * LANE] = jnp.concatenate(
+                            [mixed, jnp.zeros((BLK, LANE - 2 * width), jnp.float32)], axis=1
+                        ).astype(jnp.bfloat16)
 
     swap_wait(*state_swap(0, False))
     early = own_sweep(state.at[0])
@@ -717,6 +728,7 @@
     swap_start(*pack_swap(4))
     swap_start(*row_swap(base_bias, 5))
     matrices()
+    solve_known()
     swap_wait(*fold_swap(*near_first))
     swap_wait(*fold_swap(*near_next))
     swap_wait(*fold_swap(*near_rest))
@@ -767,6 +779,7 @@
     last_steps(1, 5)
     swap_start(*state_swap(5, True))
     shell_terms(1)
+    solve_known()
     swap_wait(*state_swap(5, True))
     three_steps(1, 5)
     last = send_forces(1, 6)
@@ -873,6 +886,8 @@
             pltpu.VMEM((ROWS, LANE), f32),
             pltpu.VMEM((BLK * ROWS, LANE), f32),
             pltpu.VMEM((piece, BLK, 2 * LANE), bf16),
+            pltpu.VMEM((piece, BLK, 2 * LANE), bf16),
+            pltpu.VMEM((piece, LANE), f32),
             pltpu.VMEM((ITERS, shell_total, LANE), f32),
             pltpu.VMEM((ITERS, total, piece, LANE), f32),
             pltpu.VMEM((ITERS, piece, LANE), f32),

time: 49.9 us -> 49.7 us (level)
  no operation moved by 1% of the time
where the time goes in v6:
time: 49.7 us; the launch traced here: 49.4 us
  Pallas kernels  48.1 us (97%)
  between operations  1.29 us (3%)
    pallas_call x1, Pallas kernels, body(): pl.pallas_call(functools.partial(kernel, fluid_n, struct_n, piece), out_s...  46.7 us
    pallas_call x1, Pallas kernels, body(): pl.pallas_call(finish, out_shape=(jax.ShapeDtypeStruct((NVAR, cells), f32...  1.41 us

profile of v6, /device:TPU:0, one launch (start us, length us, event | category | flops | bytes accessed | tf_op | source)
XLA Modules:
  0.0 49.4 jit_solution(5260965171448927761)
XLA Ops:
  1.3 46.7 %shard_map.167 = (f32[5,512]{1,0:T(8,128)}, f32[32,128]{1,0:T(8,128)}) custom-call(f32[5,512]{1,0:T(8,128)} %adj_far.1, f32[5,512]{1,0:T(8,128)} %rhs_far.1, f32[5,5,512]{2,1,0:T(8,128)} %diag_far.1, f32[5,5,6,512]{3,2,1,0:T(8,128)} %bitcast.8, s32[6,512]{1,0:T(8,128)} %index_far.1, s32[1,256]{1,0:T(1,128)} %bitcast.12, s32[1,1]{1,0:T(1,128)} %bitcast.7.count_ref, ...), custom_call_target="tpu_custom_call" | custom-call | tf_op jit(solution)/shard_map/pallas_call | solution.py:851
  48.0 1.4 %shard_map.168 = (f32[5,512]{1,0:T(8,128)}, f32[24,128]{1,0:T(8,128)}) custom-call(f32[5,512]{1,0:T(8,128)} %get-tuple-element.6.fluid_in, f32[32,128]{1,0:T(8,128)} %get-tuple-element.7.struct_in), custom_call_target="tpu_custom_call" | custom-call | tf_op jit(solution)/shard_map/pallas_call | solution.py:943
